TPU v7x, 512 devices: a whole 4x4x16 slice. The times are simulated.
512 devices in a mesh: seq: 64 (over x, z_lo, core), head: 4 (over y), rep: 2 (over z_hi).
Axes of the slice: x: 4, y: 4, z: 16 (z_hi: 2, z_lo: 8; z = z_hi * 8 + z_lo), core: 2. Of those that a mesh axis runs over, the one named last changes fastest.
Arguments:
- token_ids: int32 [32768], P(('rep', 'seq')), parts along dimension 0, may hold values from 0 to 15
- embedding: float32 [16, 256], replicated, may hold values from -6 to 6
- complement: int32 [256], replicated, may hold values from 0 to 255, each once
- prenorm_first: float32 [256], replicated, may hold values from 0.1 to 1.9
- inproj_first: float32 [256, 2, 512], P(None, None, 'head'), may hold values from -0.375 to 0.375
- statemap_first: float32 [256, 2, 128], replicated, may hold values from -0.375 to 0.375
- stepmap_first: float32 [256, 8], P(None, 'head'), may hold values from -0.375 to 0.375
- stepbias_first: float32 [8], P('head'), may hold values from -1 to 1
- rates_first: float32 [8], P('head'), may hold values from 1.15966797e-05 to 0.11, as said below
- skipgain_first: float32 [8], P('head'), may hold values from 0.5 to 1.5
- outnorm_first: float32 [512], P('head'), may hold values from 0.1 to 1.9
- outproj_first: float32 [512, 256], P('head'), may hold values from -0.25 to 0.25
- prenorm_second: float32 [256], replicated, may hold values from 0.1 to 1.9
- inproj_second: float32 [256, 2, 512], P(None, None, 'head'), may hold values from -0.375 to 0.375
- statemap_second: float32 [256, 2, 128], replicated, may hold values from -0.375 to 0.375
- stepmap_second: float32 [256, 8], P(None, 'head'), may hold values from -0.375 to 0.375
- stepbias_second: float32 [8], P('head'), may hold values from -1 to 1
- rates_second: float32 [8], P('head'), may hold values from 1.15966797e-05 to 0.11, as said below
- skipgain_second: float32 [8], P('head'), may hold values from 0.5 to 1.5
- outnorm_second: float32 [512], P('head'), may hold values from 0.1 to 1.9
- outproj_second: float32 [512, 256], P('head'), may hold values from -0.25 to 0.25
Outputs:
- strand_out: float32 [32768, 256], P(('rep', 'seq', 'head')), parts along dimension 0
There are 2 independent parts, one for each index of `rep`. A program takes and returns all parts, laid end to end along the dimension named above; an argument that names none is the same for every part. Nothing has to cross between parts.
Inputs may be any that keep to these rules, and one draw needn't show every extreme that they name: `complement`: each channel index appears once. `rates_first`: positive rates. `rates_second`: positive rates.
All inputs are finite; a program needn't handle non-finite values.
Results may differ from a plain program's by a relative error of at most 0.00018.
Values sent between devices are 32-bit elements; how exact they have to be, the bound alone decides.
A program may use at most 64 MiB of HBM per device.

v0:
```python
import jax
import jax.numpy as jnp
from jax import lax
from jax.sharding import Mesh
from jax.sharding import PartitionSpec as P

BLOCK = 256
SEQ = ("seq_0", "seq_1", "seq_2")
REP_SEQ = ("rep", "seq_0", "seq_1", "seq_2")
REP_SEQ_HEAD = ("rep", "seq_0", "seq_1", "seq_2", "head")


highest = lax.Precision.HIGHEST
epsilon = 1e-05


def nothing_yet(array, identity):
    return jax.tree.map(
        lambda a, e: jnp.broadcast_to(jnp.asarray(e, a.dtype), a.shape), array, identity
    )


def gathered_once(array, axis):
    leaves = jax.tree.leaves(array)
    turns = sorted(range(len(leaves)), key=lambda k: -leaves[k].size)
    width = (1, *leaves[turns[0]].shape)[-1]
    lines = [
        jnp.pad(leaves[k].reshape(-1), (0, -leaves[k].size % width)).reshape(-1, width)
        for k in turns
    ]
    both, at, found = (lax.all_gather(jnp.concatenate(lines), axis), 0, {})
    for k, line in zip(turns, lines):
        piece = both[:, at : at + len(line)].reshape(len(both), -1)
        found[k] = piece[:, : leaves[k].size].reshape(-1, *leaves[k].shape)
        at += len(line)
    numbers = iter(range(len(leaves)))
    return jax.tree.map(lambda _: found[next(numbers)], array)


def prefix_by_axis(array, axes, combine, identity, reverse):
    before = start = nothing_yet(array, identity)
    running = array
    for axis in reversed(axes):
        count, position = (lax.axis_size(axis), lax.axis_index(axis))
        pieces = gathered_once(running, axis)
        inside, running = (start, start)
        for k in reversed(range(count)) if reverse else range(count):
            passed = k > position if reverse else k < position
            running = combine(running, jax.tree.map(lambda part: part[k], pieces))
            inside = jax.tree.map(lambda new, old: jnp.where(passed, new, old), running, inside)
        before = combine(inside, before)
    return before


def cut_along(array, dim, count):
    before, after = (array.shape[:dim], array.shape[dim + 1 :])
    return jnp.moveaxis(array.reshape(*before, count, -1, *after), dim, 0)


def sum_at_owner(array, axis, dim):
    count = lax.axis_size(axis)
    parts = lax.all_to_all(cut_along(array, dim, count), axis, 0, 0, tiled=True)
    return jnp.sum(parts, axis=0)


def partner(value, axis, apart):
    mask = 2**apart
    pairs = [(source, source ^ mask) for source in range(lax.axis_size(axis))]
    return lax.ppermute(value, axis, pairs)


def in_order(parts, dim):
    dims = list(parts.shape[1:])
    dims[dim] *= parts.shape[0]
    return jnp.moveaxis(parts, 0, dim).reshape(dims)


def sent_to_all(array, axis):
    count = lax.axis_size(axis)
    return lax.all_to_all(
        jnp.broadcast_to(array[None], (count, *array.shape)), axis, 0, 0, tiled=True
    )


def gathered_copies(array, axis, dim):
    return in_order(sent_to_all(array, axis), dim)


def matmul(left, right):
    return jnp.dot(left, right, precision=highest, preferred_element_type=jnp.float32)


def rms_scale(values, gain_vec):
    return (
        values * lax.rsqrt(jnp.mean(values * values, axis=-1, keepdims=True) + epsilon) * gain_vec
    )


def running(values, axis_number, reverse):
    if reverse:
        return jnp.flip(jnp.cumsum(jnp.flip(values, axis_number), axis_number), axis_number)
    return jnp.cumsum(values, axis_number)


def project(layer_in, prenorm, inproj, statemap, stepmap, stepbias, rates):
    normed = rms_scale(layer_in, prenorm)
    length = layer_in.shape[0]
    inner_width = inproj.shape[2]
    head_count = stepmap.shape[1]
    both_parts = matmul(normed, inproj.reshape(inproj.shape[0], 2 * inner_width))
    gate_vals = both_parts[:, :inner_width]
    x_heads = both_parts[:, inner_width:].reshape(length, head_count, inner_width // head_count)
    state_width = statemap.shape[2]
    write_read = matmul(normed, statemap.reshape(statemap.shape[0], 2 * state_width))
    write_vecs = write_read[:, :state_width]
    read_vecs = write_read[:, state_width:]
    step_sizes = jax.nn.softplus(matmul(normed, stepmap) + stepbias)
    log_decay = -rates * step_sizes
    return (gate_vals, x_heads, write_vecs, read_vecs, step_sizes, log_decay)


def gated_norm(outputs, gate_vals, outnorm):
    length, head_count, head_dim = outputs.shape
    gated_vals = outputs * jax.nn.silu(gate_vals).reshape(outputs.shape)
    normed = gated_vals * lax.rsqrt(
        jnp.mean(gated_vals * gated_vals, axis=-1, keepdims=True) + epsilon
    )
    return normed.reshape(length, head_count * head_dim) * outnorm


def pair_products(write_vecs, read_vecs):
    blocks = write_vecs.shape[0] // BLOCK
    return jnp.einsum(
        "kqn,ksn->kqs",
        read_vecs.reshape(blocks, BLOCK, -1),
        write_vecs.reshape(blocks, BLOCK, -1),
        precision=highest,
    )


def combine(earlier, latter):
    return (earlier[0] * latter[0], latter[0][:, None, None] * earlier[1] + latter[1])


def state_space(x_heads, step_sizes, log_decay, write_vecs, read_vecs, products, skipgain, reverse):
    length, head_count, head_dim = x_heads.shape
    blocks = length // BLOCK
    x_blocks = x_heads.reshape(blocks, BLOCK, head_count, head_dim)
    step_blocks = step_sizes.reshape(blocks, BLOCK, head_count).transpose(0, 2, 1)
    log_blocks = log_decay.reshape(blocks, BLOCK, head_count).transpose(0, 2, 1)
    write_blocks = write_vecs.reshape(blocks, BLOCK, -1)
    read_blocks = read_vecs.reshape(blocks, BLOCK, -1)
    cumulative = running(log_blocks, 2, reverse)
    differ = cumulative[:, :, :, None] - cumulative[:, :, None, :]
    positions = jnp.arange(BLOCK)
    if reverse:
        allowed = positions[None, :] >= positions[:, None]
        end_log = cumulative[:, :, 0]
    else:
        allowed = positions[None, :] <= positions[:, None]
        end_log = cumulative[:, :, -1]
    weights = (
        jnp.where(allowed, jnp.exp(jnp.where(allowed, differ, 0.0)), 0.0)
        * products[:, None]
        * step_blocks[:, :, None, :]
    )
    intra = jnp.einsum("khqs,kshp->kqhp", weights, x_blocks, precision=highest)
    scaled = (
        x_blocks
        * (jnp.exp(end_log[:, :, None] - cumulative) * step_blocks).transpose(0, 2, 1)[
            :, :, :, None
        ]
    )
    states = jnp.einsum("kshp,ksn->khpn", scaled, write_blocks, precision=highest)

    def block_step(carry_state, item_pair):
        decay_now, state_now = item_pair
        return (decay_now[:, None, None] * carry_state + state_now, carry_state)

    local_end, entering = lax.scan(
        block_step,
        jnp.zeros(states.shape[1:], jnp.float32),
        (jnp.exp(end_log), states),
        reverse=reverse,
    )
    prior_log = running(end_log, 0, reverse) - end_log
    decay_total = jnp.exp(jnp.sum(end_log, axis=0))
    identity = (jnp.ones_like(decay_total), jnp.zeros_like(local_end))
    if reverse:
        carried = prefix_by_axis((decay_total, local_end), SEQ, combine, identity, True)[1]
    else:
        carried = prefix_by_axis((decay_total, local_end), SEQ, combine, identity, False)[1]
    entering = entering + jnp.exp(prior_log)[:, :, None, None] * carried[None]
    inter = (
        jnp.einsum("kqn,khpn->kqhp", read_blocks, entering, precision=highest)
        * jnp.exp(cumulative).transpose(0, 2, 1)[:, :, :, None]
    )
    outputs = intra + inter + skipgain[None, None, :, None] * x_blocks
    return outputs.reshape(length, head_count, head_dim)


def per_device(
    token_ids,
    embedding,
    complement,
    prenorm_first,
    inproj_first,
    statemap_first,
    stepmap_first,
    stepbias_first,
    rates_first,
    skipgain_first,
    outnorm_first,
    outproj_first,
    prenorm_second,
    inproj_second,
    statemap_second,
    stepmap_second,
    stepbias_second,
    rates_second,
    skipgain_second,
    outnorm_second,
    outproj_second,
):
    onehot = (
        token_ids[:, None] == jnp.arange(embedding.shape[0], dtype=jnp.int32)[None, :]
    ).astype(jnp.float32)
    embedded = matmul(onehot, embedding)
    gate_vals, x_heads, write_vecs, read_vecs, step_sizes, log_decay = project(
        embedded,
        prenorm_first,
        inproj_first,
        statemap_first,
        stepmap_first,
        stepbias_first,
        rates_first,
    )
    products = pair_products(write_vecs, read_vecs)
    forward_out = state_space(
        x_heads, step_sizes, log_decay, write_vecs, read_vecs, products, skipgain_first, False
    )
    backward_out = state_space(
        x_heads, step_sizes, log_decay, write_vecs, read_vecs, products, skipgain_first, True
    )
    mixed = gated_norm(forward_out, gate_vals, outnorm_first) + gated_norm(
        backward_out, gate_vals, outnorm_first
    )
    partial_sum = matmul(mixed, outproj_first)
    bit_count = lax.axis_size(SEQ).bit_length() - 1
    share = sum_at_owner(partial_sum, "head", 0)
    share_rows = share.shape[0]
    moved = (
        lax.dynamic_slice_in_dim(embedded, lax.axis_index("head") * share_rows, share_rows, 0)
        + share
    )
    for bit_index in range(bit_count):
        moved = partner(moved, SEQ, bit_index)
    moved = gathered_copies(moved, "head", 0)
    flipped = moved[::-1]
    mirrored = jnp.take(flipped, complement, axis=1)
    gate_two, x_two, write_two, read_two, step_two, log_two = project(
        mirrored,
        prenorm_second,
        inproj_second,
        statemap_second,
        stepmap_second,
        stepbias_second,
        rates_second,
    )
    products_two = pair_products(write_two, read_two)
    forward_two = state_space(
        x_two, step_two, log_two, write_two, read_two, products_two, skipgain_second, False
    )
    partial_two = matmul(gated_norm(forward_two, gate_two, outnorm_second), outproj_second)
    share_two = sum_at_owner(partial_two, "head", 0)
    rows_two = share_two.shape[0]
    return (
        lax.dynamic_slice_in_dim(mirrored, lax.axis_index("head") * rows_two, rows_two, 0)
        + share_two
    )


def solution(mesh):
    finer = Mesh(
        mesh.devices.reshape(4, 8, 2, mesh.shape["head"], mesh.shape["rep"]),
        ("seq_0", "seq_1", "seq_2", "head", "rep"),
    )
    in_specs = (
        P(REP_SEQ),
        P(),
        P(),
        P(),
        P(None, None, "head"),
        P(),
        P(None, "head"),
        P("head"),
        P("head"),
        P("head"),
        P("head"),
        P("head", None),
        P(),
        P(None, None, "head"),
        P(),
        P(None, "head"),
        P("head"),
        P("head"),
        P("head"),
        P("head"),
        P("head", None),
    )
    out_specs = P(REP_SEQ_HEAD, None)
    return jax.shard_map(
        per_device, mesh=finer, in_specs=in_specs, out_specs=out_specs, check_vma=False
    )
```

profile of v0, /device:TPU:6, one launch (start us, length us, event | category | flops | bytes accessed | tf_op | source)
XLA Modules:
  0.0 306.7 jit_solution(4768765200244375174)
XLA Ops:
  0.0 1.2 multiply_reduce_fusion.1
  1.2 0.6 copy-done.15
  1.8 0.7 copy-done.8
  3.0 0.6 reduce-window.20
  4.0 0.6 reduce-window.24
  5.8 0.7 fusion.36
  6.7 0.4 fusion.33
  7.6 1.9 all-gather.9
  9.9 50.6 %all-gather.10 = f32[8,129,128]{2,1,0:T(8,128)S(1)} all-gather(f32[1,129,128]{2,1,0:T(8,128)S(1)} %maximum_bitcast_fusion.1), channel_id=3, replica_groups=mesh['seq_0'=4,'seq_1'=8,'seq_2'=2,'head'=4,'rep'=2] {'seq_1'}, dimensions={0}, use_global_device_ids=true | all-gather | bytes 594432 | tf_op jit(solution)/shard_map/all_gather | solution.py:31
  61.1 1.9 all-gather.12
  63.4 48.2 %all-gather.13 = f32[8,129,128]{2,1,0:T(8,128)S(1)} all-gather(f32[1,129,128]{2,1,0:T(8,128)S(1)} %maximum_bitcast_fusion.4), channel_id=6, replica_groups=mesh['seq_0'=4,'seq_1'=8,'seq_2'=2,'head'=4,'rep'=2] {'seq_1'}, dimensions={0}, use_global_device_ids=true | all-gather | bytes 594432 | tf_op jit(solution)/shard_map/all_gather | solution.py:31
  113.7 12.3 %all-gather.11 = f32[4,129,128]{2,1,0:T(8,128)S(1)} all-gather(f32[1,129,128]{2,1,0:T(8,128)S(1)} %maximum_bitcast_fusion.2), channel_id=4, replica_groups=mesh['seq_0'=4,'seq_1'=8,'seq_2'=2,'head'=4,'rep'=2] {'seq_0'}, dimensions={0}, use_global_device_ids=true | all-gather | bytes 330240 | tf_op jit(solution)/shard_map/all_gather | solution.py:31
  128.5 12.3 %all-gather.14 = f32[4,129,128]{2,1,0:T(8,128)S(1)} all-gather(f32[1,129,128]{2,1,0:T(8,128)S(1)} %maximum_bitcast_fusion.5), channel_id=7, replica_groups=mesh['seq_0'=4,'seq_1'=8,'seq_2'=2,'head'=4,'rep'=2] {'seq_0'}, dimensions={0}, use_global_device_ids=true | all-gather | bytes 330240 | tf_op jit(solution)/shard_map/all_gather | solution.py:31
  140.8 0.6 mul.1738
  141.5 0.8 mul.1739
  142.2 0.6 mul.1742
  142.9 0.8 mul.1743
  143.6 0.6 mul.1746
  144.3 0.8 mul.1747
  145.0 0.6 mul.1751
  145.6 0.8 mul.1752
  146.4 0.6 mul.1702
  147.0 0.8 mul.1703
  147.8 0.6 mul.1758
  148.4 0.8 mul.1759
  149.2 0.6 mul.1670
  149.8 0.8 mul.1671
  151.9 0.6 copy-done.16
  152.6 0.8 fusion.6
  153.3 0.8 fusion.73
  154.2 0.6 copy-done.12
  155.0 1.1 fusion.66
  156.1 4.5 %all-to-all-start = ((f32[4,64,256]{2,1,0:T(8,128)}), f32[4,64,256]{2,1,0:T(8,128)S(1)}, u32[]{:S(2)}, u32[]{:S(2)}) async-start(f32[4,64,256]{2,1,0:T(8,128)} %fusion.66), calls=%async_computation | async-start | bytes 524288 | tf_op jit(solution)/shard_map/all_to_all | solution.py:62
  160.5 6.7 %all-to-all-done = f32[4,64,256]{2,1,0:T(8,128)S(1)} async-done(((f32[4,64,256]{2,1,0:T(8,128)}), f32[4,64,256]{2,1,0:T(8,128)S(1)}, u32[]{:S(2)}, u32[]{:S(2)}) %all-to-all-start) | async-done | bytes 262176 | tf_op jit(solution)/shard_map/all_to_all | solution.py:62
  167.3 1.9 collective-permute-start
  169.2 1.2 collective-permute-done
  170.4 4.2 %collective-permute-start.1 = (f32[64,256]{1,0:T(8,128)S(1)}, f32[64,256]{1,0:T(8,128)S(1)}, u32[]{:S(2)}, u32[]{:S(2)}) collective-permute-start(f32[64,256]{1,0:T(8,128)S(1)} %collective-permute-done), channel_id=1, source_target_pairs={{0,16},{8,24},{16,0},{24,8},{32,48},{40,56},{48,32},{56,40},{64,80... | collective-permute-start | bytes 196616 | tf_op jit(solution)/shard_map/ppermute | solution.py:69
  174.6 2.4 collective-permute-done.1
  177.0 1.9 collective-permute-start.2
  178.9 5.2 %collective-permute-done.2 = f32[64,256]{1,0:T(8,128)S(1)} collective-permute-done((f32[64,256]{1,0:T(8,128)S(1)}, f32[64,256]{1,0:T(8,128)S(1)}, u32[]{:S(2)}, u32[]{:S(2)}) %collective-permute-start.2) | collective-permute-done | bytes 65568 | tf_op jit(solution)/shard_map/ppermute | solution.py:69
  184.1 7.1 %collective-permute-start.3 = (f32[64,256]{1,0:T(8,128)S(1)}, f32[64,256]{1,0:T(8,128)S(1)}, u32[]{:S(2)}, u32[]{:S(2)}) collective-permute-start(f32[64,256]{1,0:T(8,128)S(1)} %collective-permute-done.2), channel_id=1, source_target_pairs={{0,64},{8,72},{16,80},{24,88},{32,96},{40,104},{48,112},{56,120},{... | collective-permute-start | bytes 196616 | tf_op jit(solution)/shard_map/ppermute | solution.py:69
  191.2 5.1 %collective-permute-done.3 = f32[64,256]{1,0:T(8,128)S(1)} collective-permute-done((f32[64,256]{1,0:T(8,128)S(1)}, f32[64,256]{1,0:T(8,128)S(1)}, u32[]{:S(2)}, u32[]{:S(2)}) %collective-permute-start.3) | collective-permute-done | bytes 65568 | tf_op jit(solution)/shard_map/ppermute | solution.py:69
  196.3 2.4 collective-permute-start.4
  198.7 3.7 %collective-permute-done.4 = f32[64,256]{1,0:T(8,128)S(1)} collective-permute-done((f32[64,256]{1,0:T(8,128)S(1)}, f32[64,256]{1,0:T(8,128)S(1)}, u32[]{:S(2)}, u32[]{:S(2)}) %collective-permute-start.4) | collective-permute-done | bytes 65568 | tf_op jit(solution)/shard_map/ppermute | solution.py:69
  202.4 3.8 %collective-permute-start.5 = (f32[64,256]{1,0:T(8,128)S(1)}, f32[64,256]{1,0:T(8,128)S(1)}, u32[]{:S(2)}, u32[]{:S(2)}) collective-permute-start(f32[64,256]{1,0:T(8,128)S(1)} %collective-permute-done.4), channel_id=1, source_target_pairs={{0,256},{8,264},{16,272},{24,280},{32,288},{40,296},{48,304},{56,3... | collective-permute-start | bytes 196616 | tf_op jit(solution)/shard_map/ppermute | solution.py:69
  206.2 3.8 %collective-permute-done.5 = f32[64,256]{1,0:T(8,128)S(1)} collective-permute-done((f32[64,256]{1,0:T(8,128)S(1)}, f32[64,256]{1,0:T(8,128)S(1)}, u32[]{:S(2)}, u32[]{:S(2)}) %collective-permute-start.5) | collective-permute-done | bytes 65568 | tf_op jit(solution)/shard_map/ppermute | solution.py:69
  210.1 0.7 broadcast_in_dim.58
  210.8 3.4 %all-to-all-start.1 = ((f32[4,64,256]{2,1,0:T(8,128)}), f32[4,64,256]{2,1,0:T(8,128)S(1)}, u32[]{:S(2)}, u32[]{:S(2)}) async-start(f32[4,64,256]{2,1,0:T(8,128)} %broadcast_in_dim.58), calls=%async_computation.1 | async-start | bytes 524288 | tf_op jit(solution)/shard_map/all_to_all | solution.py:80
  214.2 6.6 %all-to-all-done.1 = f32[4,64,256]{2,1,0:T(8,128)S(1)} async-done(((f32[4,64,256]{2,1,0:T(8,128)}), f32[4,64,256]{2,1,0:T(8,128)S(1)}, u32[]{:S(2)}, u32[]{:S(2)}) %all-to-all-start.1) | async-done | bytes 262176 | tf_op jit(solution)/shard_map/all_to_all | solution.py:80
  221.3 1.0 gather_fusion
  222.6 0.5 copy-done.7
  223.7 0.6 reduce-window.26
  225.1 0.4 fusion.27
  225.5 0.5 copy-done.4
  226.0 0.7 fusion.30
  227.2 1.9 all-gather.15
  229.5 48.0 %all-gather.16 = f32[8,129,128]{2,1,0:T(8,128)S(1)} all-gather(f32[1,129,128]{2,1,0:T(8,128)S(1)} %maximum_bitcast_fusion.7), channel_id=9, replica_groups=mesh['seq_0'=4,'seq_1'=8,'seq_2'=2,'head'=4,'rep'=2] {'seq_1'}, dimensions={0}, use_global_device_ids=true | all-gather | bytes 594432 | tf_op jit(solution)/shard_map/all_gather | solution.py:31
  279.4 12.3 %all-gather.17 = f32[4,129,128]{2,1,0:T(8,128)S(1)} all-gather(f32[1,129,128]{2,1,0:T(8,128)S(1)} %maximum_bitcast_fusion.8), channel_id=10, replica_groups=mesh['seq_0'=4,'seq_1'=8,'seq_2'=2,'head'=4,'rep'=2] {'seq_0'}, dimensions={0}, use_global_device_ids=true | all-gather | bytes 330240 | tf_op jit(solution)/shard_map/all_gather | solution.py:31
  293.4 0.6 copy-done.18
  294.1 0.8 fusion.64
  294.9 0.6 copy-done.14
  295.8 0.8 copy-done.5
  296.9 9.1 %all_to_all.15 = f32[4,64,256]{2,1,0:T(8,128)S(1)} all-to-all(f32[4,64,256]{2,1,0:T(8,128)S(1)} %fusion.60), channel_id=1, replica_groups=mesh['seq_0'=4,'seq_1'=8,'seq_2'=2,'head'=4,'rep'=2] {'head'}, dimensions={0} | all-to-all | bytes 524288 | tf_op jit(solution)/shard_map/all_to_all | solution.py:62
  306.0 0.6 bitcast_add_fusion.10
  (252 shorter events, 17.2 us)
Async XLA Ops:
  0.0 155.0 %copy-start = (f32[128,256]{1,0:T(8,128)S(1)}, f32[128,256]{1,0:T(8,128)}, u32[]{:S(2)}) copy-start(f32[128,256]{1,0:T(8,128)} %param.32) | copy-start | bytes 393220
  0.0 5.8 %copy-start.1 = (f32[256,2,128]{2,1,0:T(2,128)S(1)}, f32[256,2,128]{2,1,0:T(2,128)}, u32[]{:S(2)}) copy-start(f32[256,2,128]{2,1,0:T(2,128)} %param.25) | copy-start | bytes 786436
  1.2 0.7 copy-start.15
  1.8 0.7 copy-start.8
  1.8 0.7 copy-start.6
  1.8 0.7 copy-start.11
  5.8 1.0 copy-start.2
  151.9 0.7 copy-start.16
  154.2 0.7 copy-start.12
  156.1 11.1 %all-to-all-start = ((f32[4,64,256]{2,1,0:T(8,128)}), f32[4,64,256]{2,1,0:T(8,128)S(1)}, u32[]{:S(2)}, u32[]{:S(2)}) async-start(f32[4,64,256]{2,1,0:T(8,128)} %fusion.66), calls=%async_computation | async-start | bytes 524288 | tf_op jit(solution)/shard_map/all_to_all | solution.py:62
  167.2 31.4 %copy-start.10 = (s32[256]{0:T(256)S(1)}, s32[256]{0:T(256)}, u32[]{:S(2)}) copy-start(s32[256]{0:T(256)} %param.23) | copy-start | bytes 3076
  167.3 31.4 %copy-start.17 = (f32[2]{0:T(128)S(1)}, f32[2]{0:T(128)}, u32[]{:S(2)}) copy-start(f32[2]{0:T(128)} %param.38) | copy-start | bytes 28
  167.3 3.1 %collective-permute-start = (f32[64,256]{1,0:T(8,128)S(1)}, f32[64,256]{1,0:T(8,128)S(1)}, u32[]{:S(2)}, u32[]{:S(2)}) collective-permute-start(f32[64,256]{1,0:T(8,128)S(1)} %dynamic-slice_add_fusion), channel_id=1, source_target_pairs={{0,8},{8,0},{16,24},{24,16},{32,40},{40,32},{48,56},{56,48},{64,72... | collective-permute-start | bytes 196616 | tf_op jit(solution)/shard_map/ppermute | solution.py:69
  170.4 6.6 %collective-permute-start.1 = (f32[64,256]{1,0:T(8,128)S(1)}, f32[64,256]{1,0:T(8,128)S(1)}, u32[]{:S(2)}, u32[]{:S(2)}) collective-permute-start(f32[64,256]{1,0:T(8,128)S(1)} %collective-permute-done), channel_id=1, source_target_pairs={{0,16},{8,24},{16,0},{24,8},{32,48},{40,56},{48,32},{56,40},{64,80... | collective-permute-start | bytes 196616 | tf_op jit(solution)/shard_map/ppermute | solution.py:69
  177.0 7.1 %collective-permute-start.2 = (f32[64,256]{1,0:T(8,128)S(1)}, f32[64,256]{1,0:T(8,128)S(1)}, u32[]{:S(2)}, u32[]{:S(2)}) collective-permute-start(f32[64,256]{1,0:T(8,128)S(1)} %collective-permute-done.1), channel_id=1, source_target_pairs={{0,32},{8,40},{16,48},{24,56},{32,0},{40,8},{48,16},{56,24},{64,96... | collective-permute-start | bytes 196616 | tf_op jit(solution)/shard_map/ppermute | solution.py:69
  184.1 12.2 %collective-permute-start.3 = (f32[64,256]{1,0:T(8,128)S(1)}, f32[64,256]{1,0:T(8,128)S(1)}, u32[]{:S(2)}, u32[]{:S(2)}) collective-permute-start(f32[64,256]{1,0:T(8,128)S(1)} %collective-permute-done.2), channel_id=1, source_target_pairs={{0,64},{8,72},{16,80},{24,88},{32,96},{40,104},{48,112},{56,120},{... | collective-permute-start | bytes 196616 | tf_op jit(solution)/shard_map/ppermute | solution.py:69
  196.3 6.1 %collective-permute-start.4 = (f32[64,256]{1,0:T(8,128)S(1)}, f32[64,256]{1,0:T(8,128)S(1)}, u32[]{:S(2)}, u32[]{:S(2)}) collective-permute-start(f32[64,256]{1,0:T(8,128)S(1)} %collective-permute-done.3), channel_id=1, source_target_pairs={{0,128},{8,136},{16,144},{24,152},{32,160},{40,168},{48,176},{56,1... | collective-permute-start | bytes 196616 | tf_op jit(solution)/shard_map/ppermute | solution.py:69
  202.4 7.7 %collective-permute-start.5 = (f32[64,256]{1,0:T(8,128)S(1)}, f32[64,256]{1,0:T(8,128)S(1)}, u32[]{:S(2)}, u32[]{:S(2)}) collective-permute-start(f32[64,256]{1,0:T(8,128)S(1)} %collective-permute-done.4), channel_id=1, source_target_pairs={{0,256},{8,264},{16,272},{24,280},{32,288},{40,296},{48,304},{56,3... | collective-permute-start | bytes 196616 | tf_op jit(solution)/shard_map/ppermute | solution.py:69
  210.8 10.1 %all-to-all-start.1 = ((f32[4,64,256]{2,1,0:T(8,128)}), f32[4,64,256]{2,1,0:T(8,128)S(1)}, u32[]{:S(2)}, u32[]{:S(2)}) async-start(f32[4,64,256]{2,1,0:T(8,128)} %broadcast_in_dim.58), calls=%async_computation.1 | async-start | bytes 524288 | tf_op jit(solution)/shard_map/all_to_all | solution.py:80
  222.4 0.7 copy-start.7
  222.5 0.7 copy-start.9
  222.5 0.7 copy-start.13
  222.6 2.5 copy-start.3
  225.1 1.0 copy-start.4
  293.4 0.7 copy-start.18
  294.9 0.7 copy-start.14
  295.7 0.9 copy-start.5
where the time goes:
time: 308 us; the launch traced here: 307 us
  blocking collectives  198 us (64%)
  waiting for transfers between devices  34.7 us (11%)
  starting transfers between devices  29.1 us (9%)
  local copies, waits for them, and re-layouts  27.2 us (9%)
  matrix products  10.3 us (3%)
  other arithmetic  5.99 us (2%)
    all_gather x9, blocking collectives, gathered_once(): both, at, found = (lax.all_gather(jnp.concatenate(lines), axis), 0, {})  189 us
    ppermute x6, waiting for transfers between devices, partner(): return lax.ppermute(value, axis, pairs)  21.4 us
    ppermute x6, starting transfers between devices, partner(): return lax.ppermute(value, axis, pairs)  21.3 us
    mul x99, local copies, waits for them, and re-layouts, combine(): latter[0][:, None, None] * earlier[1] + latter[1]  14.8 us
    all_to_all x1, blocking collectives, sum_at_owner(): parts = lax.all_to_all(cut_along(array, dim, count), axis, 0, 0, tiled=True)  9.07 us
    all_to_all x1, waiting for transfers between devices, sum_at_owner(): parts = lax.all_to_all(cut_along(array, dim, count), axis, 0, 0, tiled=True)  6.68 us
    all_to_all x1, waiting for transfers between devices, sent_to_all(): lax.all_to_all(jnp.broadcast_to(array[None], (count, *array.shape)), axis...  6.63 us
  transfers between devices with their start and end apart: 8, of which 8 were waited for; matrix products, arithmetic and copies ran while one was open for 0% of the time, Pallas kernels for 0%

commit v1 on v0

v1 whole, which is shorter than its diff:
```python
import jax
import jax.numpy as jnp
from jax import lax
from jax.experimental import pallas as pl
from jax.experimental.pallas import tpu as pltpu
from jax.sharding import PartitionSpec as P

F32, BF = jnp.float32, jnp.bfloat16
MESH = pl.DeviceIdType.MESH
EPS = 1e-05
NX, NZ, NC, NY = 4, 8, 2, 4
T = 256
V = 16


def mm(a, b):
    return lax.dot_general(a, b, (((1,), (0,)), ((), ())), preferred_element_type=F32)


def mmt(a, b):
    return lax.dot_general(a, b, (((1,), (1,)), ((), ())), preferred_element_type=F32)


def split2(a):
    hi = a.astype(BF)
    return hi, (a - hi.astype(F32)).astype(BF)


def split3(a):
    hi = a.astype(BF)
    rest = a - hi.astype(F32)
    mid = rest.astype(BF)
    return hi, mid, (rest - mid.astype(F32)).astype(BF)


def dot3(a, b, f=mm):
    ah, al = a if isinstance(a, tuple) else split2(a)
    bh, bl = b if isinstance(b, tuple) else split2(b)
    return f(ah, bh) + (f(ah, bl) + f(al, bh))


def exact_left(a, b):
    h, m, l = split3(b)
    return mm(a, h) + (mm(a, m) + mm(a, l))


def exact_right(a, b):
    h, m, l = split3(a)
    return mm(h, b) + (mm(m, b) + mm(l, b))


def iota(shape, dim):
    return lax.broadcasted_iota(jnp.int32, shape, dim)


def softplus(a):
    return jnp.maximum(a, 0.0) + jnp.log1p(jnp.exp(-jnp.abs(a)))


def silu(a):
    return a / (1.0 + jnp.exp(-a))


def rms(a, gain):
    return a * lax.rsqrt(jnp.mean(a * a, axis=-1, keepdims=True) + EPS) * gain


def xor(a, k, bits):
    out = a
    for i in range(bits):
        if k >> i & 1:
            out = out + (1 << i) * (1 - 2 * (a // (1 << i) % 2))
    return out


def pick(flag, a, b):
    return jnp.where(jnp.full(a.shape, flag, jnp.int32) > 0, a, b)


def as_int(cond):
    return jnp.where(cond, 1, 0)


def halves(pair):
    return jnp.where(iota((1, 128), 1) < 64, pair[:, 0:1], pair[:, 1:2])


def scan_rows(coef, decay, reverse):
    rows = iota(coef.shape, 0)
    k = 1
    while k < T:
        if reverse:
            inside = rows < T - k
            shifted_c, shifted_d = pltpu.roll(coef, T - k, 0), pltpu.roll(decay, T - k, 0)
        else:
            inside = rows >= k
            shifted_c, shifted_d = pltpu.roll(coef, k, 0), pltpu.roll(decay, k, 0)
        coef = coef + jnp.where(inside, decay * shifted_c, 0.0)
        decay = jnp.where(inside, decay * shifted_d, decay)
        k *= 2
    return coef, decay


NAMES = (
    "tok", "emb", "comp",
    "pn1", "ip1", "sm1", "sp1", "sb1", "ra1", "sk1", "on1", "op1",
    "pn2", "ip2", "sm2", "sp2", "sb2", "ra2", "sk2", "on2", "op2",
)
SHAPES = (
    (1, T), (V, 256), (1, 256),
    (1, 256), (512, 128), (512, 128), (2, 256), (1, 2), (1, 2), (1, 2), (1, 128), (128, 256),
    (1, 256), (512, 128), (512, 128), (2, 256), (1, 2), (1, 2), (1, 2), (1, 128), (128, 256),
)
TYPES = (jnp.int32, F32, jnp.int32) + (F32,) * 18
N_IN = len(NAMES)
TAB = 80
MSG = 72

SCRATCH = (
    ("tokbuf", (8, 1, T), jnp.int32),
    ("tokm", (1, T), jnp.int32),
    ("tsend", (TAB, 128), F32),
    ("ytab", (NY, TAB, 128), F32),
    ("wo1", (NY, 128, 256), F32),
    ("wo2", (NY, 128, 256), F32),
    ("ztile", (8, 128), F32),
    ("zbuf", (NZ, 8, 128), F32),
    ("mir", (T, 256), F32),
    ("st", (128, 128), F32),
    ("e1s", (MSG, 128), F32),
    ("e1r", (MSG, 128), F32),
    ("bs", (3, MSG, 128), F32),
    ("br", (3, MSG, 128), F32),
    ("xs", (MSG, 128), F32),
    ("xr", (NX, MSG, 128), F32),
    ("ks", (64, 128), F32),
    ("kr", (64, 128), F32),
    ("gs", (T, 128), F32),
    ("gr", (NY, 64, 128), F32),
)
N_SEND = 64


def kernel(*refs):
    hbm = dict(zip(NAMES, refs[:N_IN]))
    out_ref = refs[N_IN]
    vm = dict(zip(NAMES, refs[N_IN + 1 :]))
    sc = {s[0]: r for s, r in zip(SCRATCH, refs[N_IN + 1 + N_IN :])}
    in_sem, send_sem, recv_sem = refs[-3:]

    seq, y = lax.axis_index("seq"), lax.axis_index("head")
    x, z, c = seq // (NZ * NC), seq // NC % NZ, seq % NC
    xc = x * NC + c
    xm, zm = NX - 1 - x, NZ - 1 - z

    def seq_of(xi, zi, ci):
        return (xi * NZ + zi) * NC + ci

    y_peers = [xor(y, k, 2) for k in range(1, NY)]
    xc_peers = [xor(xc, k, 3) for k in range(1, 8)]
    z_peers = [xor(z, k, 3) for k in range(1, NZ)]
    mirror = seq_of(xm, zm, 1 - c)

    barrier = pltpu.get_barrier_semaphore()

    def greet(where):
        pl.semaphore_signal(barrier, inc=1, device_id=where, device_id_type=MESH)

    for p in z_peers:
        greet({"seq": seq_of(x, p, c)})
    greet({"seq": mirror})
    for p in xc_peers:
        greet({"seq": seq_of(p // NC, z, p % NC)})
    for p in y_peers:
        greet({"head": p})

    loads = {n: pltpu.make_async_copy(hbm[n], vm[n], in_sem.at[i]) for i, n in enumerate(NAMES)}
    for n in NAMES:
        loads[n].start()
    own_tok = pltpu.make_async_copy(hbm["tok"], sc["tokbuf"].at[xc], in_sem.at[N_IN])
    own_tok.start()

    used = [0]

    def remote(src, dst, where):
        i = used[0]
        used[0] += 1
        return pltpu.make_async_remote_copy(
            src_ref=src, dst_ref=dst, send_sem=send_sem.at[i], recv_sem=recv_sem.at[i],
            device_id=where, device_id_type=MESH,
        )

    for n in NAMES:
        loads[n].wait()
    own_tok.wait()

    lane = iota((1, 128), 1)
    w1 = vm["ip1"]
    gate_w, inner_w = w1[pl.ds(0, 256, stride=2), :], w1[pl.ds(1, 256, stride=2), :]
    s1 = vm["sm1"]
    write_w, read_w = s1[pl.ds(0, 256, stride=2), :], s1[pl.ds(1, 256, stride=2), :]
    emb = vm["emb"][...]
    normed = rms(emb, vm["pn1"][...])
    normed2 = split2(normed)
    table = dot3(normed2, jnp.concatenate([gate_w, inner_w, write_w, read_w], axis=1))
    gate_t, inner_t, write_t, read_t = (table[:, 128 * i : 128 * (i + 1)] for i in range(4))
    sp = vm["sp1"][...]
    sb, ra, sk = vm["sb1"][...], vm["ra1"][...], vm["sk1"][...]
    r128 = iota((128, 256), 0)
    sp_p = jnp.where(r128 < 64, sp[0:1], sp[1:2])
    sp_alt = jnp.where(r128 // 16 % 2 == 0, sp[0:1], sp[1:2])
    logits = dot3(normed2, jnp.concatenate([sp_p, sp_alt], axis=0), mmt)
    step_p = softplus(logits[:, :128] + halves(sb))
    alt = lane // 16 % 2 == 0
    log_alt = -jnp.where(alt, ra[:, 0:1], ra[:, 1:2]) * softplus(
        logits[:, 128:] + jnp.where(alt, sb[:, 0:1], sb[:, 1:2])
    )
    even = iota((8, 128), 0) % 2 == 0
    sp_r = jnp.where(iota((8, 256), 0) % 2 == 0, sp[0:1], sp[1:2])
    log_r = -jnp.where(even, ra[:, 0:1], ra[:, 1:2]) * softplus(
        dot3(sp_r, jnp.concatenate([normed] * 8, axis=0), mmt)
        + jnp.where(even, sb[:, 0:1], sb[:, 1:2])
    )
    tsend = sc["tsend"]
    tsend[0:16] = step_p * inner_t
    tsend[16:32] = halves(sk) * inner_t
    tsend[32:48] = silu(gate_t)
    tsend[48:64] = log_alt
    tsend[64:72] = log_r
    tsend[72:80] = jnp.broadcast_to(vm["on1"][...], (8, 128))
    g_tab = dot3(read_t, jnp.concatenate([write_t] * 8, axis=0), mmt)

    pl.semaphore_wait(barrier, 18)

    ytab, tokbuf = sc["ytab"], sc["tokbuf"]
    tab_copies = [remote(tsend, ytab.at[y], {"head": p}) for p in y_peers]
    tok_copies = [
        remote(hbm["tok"], tokbuf.at[xc], {"seq": seq_of(p // NC, z, p % NC)}) for p in xc_peers
    ]
    tokm_copy = remote(hbm["tok"], sc["tokm"], {"seq": mirror})
    wo1_copies = [remote(vm["op1"], sc["wo1"].at[y], {"head": p}) for p in y_peers]
    wo2_copies = [remote(vm["op2"], sc["wo2"].at[y], {"head": p}) for p in y_peers]
    for cp in tab_copies + tok_copies + [tokm_copy] + wo1_copies + wo2_copies:
        cp.start()
    ytab[pl.ds(y, 1)] = tsend[...][None]
    sc["wo1"][pl.ds(y, 1)] = vm["op1"][...][None]
    sc["wo2"][pl.ds(y, 1)] = vm["op2"][...][None]

    tri_r, tri_c = iota((256, 256), 0), iota((256, 256), 1)
    one = jnp.ones((), F32)

    def mask_bf(cond):
        return jnp.where(cond, one, 0.0 * one).astype(BF)

    perm = mask_bf(vm["comp"][...] == tri_r)
    w2 = vm["ip2"]
    s2 = vm["sm2"]
    w2_all = split2(
        jnp.concatenate(
            [
                w2[pl.ds(0, 256, stride=2), :],
                w2[pl.ds(1, 256, stride=2), :],
                s2[pl.ds(0, 256, stride=2), :],
                s2[pl.ds(1, 256, stride=2), :],
            ],
            axis=1,
        )
    )
    sp2 = vm["sp2"][...]
    sp2_p = split2(jnp.where(r128 < 64, sp2[0:1], sp2[1:2]))
    emb_p = mm(jnp.concatenate(split3(emb), axis=0), perm).astype(BF)

    for cp in tok_copies:
        cp.wait_recv()
    for cp in tab_copies:
        cp.wait_recv()
    r16 = iota((V, T), 0)
    onehot = jnp.concatenate([as_int(tokbuf[b] == r16) for b in range(8)], axis=0)
    onehot = onehot.astype(F32).astype(BF)
    counts = mm(
        onehot,
        jnp.concatenate(
            [mask_bf(tri_r > tri_c), mask_bf(tri_r < tri_c), jnp.ones((256, 128), BF)], axis=1
        ),
    ).astype(BF)
    row8 = iota((8, 128), 0)
    log_hv = ytab[0, 64:72]
    for i in range(1, NY):
        log_hv = jnp.where(row8 // 2 == i, ytab[i, 64:72], log_hv)
    r64, l64 = iota((64, 128), 0), iota((64, 128), 1)
    log_bd = jnp.where(r64 // 8 == l64 // 16, jnp.concatenate([log_hv] * 8, axis=0), 0.0)
    cums = exact_right(log_bd, counts)
    weight = jnp.exp(cums[:, :512])
    weight = jnp.concatenate([weight[:, :256], weight[:, 256:]], axis=0)
    wh, wl = split2(weight)
    sums = mmt(wh, onehot) + mmt(wl, onehot)
    r2, l2 = iota((128, 128), 0), iota((128, 128), 1)
    sums = jnp.where(r2 // 8 % 8 == l2 // 16, sums, 0.0)
    for shift in (64, 32, 16):
        sums = sums + pltpu.roll(sums, shift, 1)
    sums = jnp.where(r2 % 8 == l2 // 16, sums, 0.0)
    totals = jnp.where(r64 % 8 == l64 // 16, cums[:, 512:], 0.0)

    def fold(a, i):
        return jnp.sum(a[8 * i : 8 * i + 8], axis=0, keepdims=True)

    cf = [fold(sums, b) for b in range(8)]
    cb = [fold(sums, 8 + b) for b in range(8)]
    ld = [fold(totals, b) for b in range(8)]
    cf_pair = [jnp.exp(ld[2 * i + 1]) * cf[2 * i] + cf[2 * i + 1] for i in range(NX)]
    cb_pair = [jnp.exp(ld[2 * i]) * cb[2 * i + 1] + cb[2 * i] for i in range(NX)]
    ld_pair = [ld[2 * i] + ld[2 * i + 1] for i in range(NX)]
    rows = [pick(as_int(xm >= i), cf_pair[i], cb_pair[i]) for i in range(NX)]
    own_b, sib, sib_ld, packed = cb_pair[0], cf[0], ld[0], ld_pair[0]
    for i in range(NX):
        here = as_int(xm == i)
        own_b = pick(here, cb_pair[i], own_b)
        sib = pick(here, pick(c, cb[2 * i + 1], cf[2 * i]), sib)
        sib_ld = pick(here, pick(c, ld[2 * i + 1], ld[2 * i]), sib_ld)
        packed = jnp.where(lane % 16 == i, ld_pair[i], packed)
    tile = jnp.concatenate(rows + [own_b, packed, sib, sib_ld], axis=0)
    ztile, zbuf = sc["ztile"], sc["zbuf"]
    ztile[...] = tile
    z_copies = [remote(ztile, zbuf.at[z], {"seq": seq_of(x, p, c)}) for p in z_peers]
    for cp in z_copies:
        cp.start()
    zbuf[pl.ds(z, 1)] = tile[None]

    def lanes_of(a, b):
        return jnp.concatenate([ytab[i, a:b] for i in range(NY)], axis=1)

    row16 = iota((V, 128), 0)
    l16 = iota((V, 128), 1)
    log_t = ytab[0, 48:64]
    for i in range(1, NY):
        log_t = jnp.where(l16 // 32 == i, ytab[i, 48:64], log_t)
    eye_t = jnp.where(row16 == l16 % 16, 1.0, 0.0)
    tables = jnp.concatenate([lanes_of(32, 48), lanes_of(16, 32), g_tab, jnp.exp(log_t), eye_t], axis=1)
    tables = jnp.concatenate([jnp.concatenate(split3(tables), axis=0), emb_p], axis=1)
    inner_rep = jnp.concatenate([lanes_of(0, 16)] * 8, axis=0)
    bd = iota((128, 512), 0) // 16 == iota((128, 512), 1) // 64
    x_bd = split2(jnp.where(bd, inner_rep, 0.0))
    outnorm_all = lanes_of(72, 73)
    tokm_copy.wait_recv()
    hot_m = as_int(sc["tokm"][...] == r16).astype(F32).astype(BF)
    rev = mask_bf(tri_r + tri_c == T - 1)
    hot_rev = mmt(rev, jnp.concatenate([hot_m] * 3, axis=0)).astype(BF)
    taken = mm(hot_rev, tables)
    silu_g, skip_x = taken[:, :512], taken[:, 512:1024]
    g_row, decay, hot = taken[:, 1024:1152], taken[:, 1152:1280], taken[:, 1280:1408]
    embedded = taken[:, 1408:]
    up_c, up_p = scan_rows(hot, decay, False)
    dn_c, dn_p = scan_rows(hot, decay, True)
    for cp in wo1_copies:
        cp.wait_recv()
    wo1h, wo1l = split2(sc["wo1"][...].reshape(512, 256))
    wo1_p = (mm(wo1h, perm).astype(BF), mm(wo1l, perm).astype(BF))

    for cp in z_copies:
        cp.wait_recv()
    ls, lr = iota((128, 512), 1), iota((128, 512), 0)
    spread = mask_bf((lr // 16 == ls % 128 // 16) & (lr % 16 == ls // 128))
    ld_all = exact_right(zbuf[:, 5, :], spread)
    ld_all = jnp.concatenate([ld_all[:, 128 * i : 128 * i + 128] for i in range(NX)], axis=0)
    qm = xm * NZ + zm
    q, q2 = iota((32, 32), 0), iota((32, 32), 1)
    between = ((q2 > q) & (q2 < qm)) | ((q2 < q) & (q2 > qm))
    share = jnp.exp(exact_left(mask_bf(between), ld_all))
    zrow = iota((8, 128), 0)
    coefs = jnp.concatenate(
        [
            jnp.where((zrow > zm) & (jnp.full((8, 128), xm, jnp.int32) == i), zbuf[:, 4, :], zbuf[:, i, :])
            for i in range(NX)
        ],
        axis=0,
    )
    terms = share * coefs
    qrow = iota((32, 128), 0)
    carry_f = jnp.sum(jnp.where(qrow < qm, terms, 0.0), axis=0, keepdims=True)
    carry_b = jnp.sum(jnp.where(qrow > qm, terms, 0.0), axis=0, keepdims=True)
    at_m = zbuf[pl.ds(zm, 1)].reshape(8, 128)
    sib, sib_d = at_m[6:7], jnp.exp(at_m[7:8])
    carry_f = pick(c, carry_f, sib_d * carry_f + sib)
    carry_b = pick(c, sib_d * carry_b + sib, carry_b)
    coef = jnp.concatenate([up_c + up_p * carry_b, dn_c + dn_p * carry_f], axis=0)
    coef = coef * jnp.concatenate([g_row] * 2, axis=0)
    ssm = dot3(coef, x_bd)

    same_head = mask_bf(r2 // 64 == l2 // 64)

    def head_scale(w):
        parts = []
        for i in range(w.shape[1] // 128):
            h, l = split2(w[:, 128 * i : 128 * i + 128] ** 2)
            parts.append(mm(h, same_head) + mm(l, same_head))
        sq = parts[0] if len(parts) == 1 else jnp.concatenate(parts, axis=1)
        return lax.rsqrt(sq * (1.0 / 64) + EPS)

    w_up = (ssm[:T] + skip_x) * silu_g
    w_dn = (ssm[T:] + skip_x) * silu_g
    mixed = (w_up * head_scale(w_up) + w_dn * head_scale(w_dn)) * outnorm_all
    mirrored = embedded + dot3(mixed, wo1_p)
    mir = sc["mir"]
    mir[...] = mirrored

    n2 = split2(rms(mirrored, vm["pn2"][...]))
    both = dot3(n2, w2_all)
    gate, inner, write, read = (both[:, 128 * i : 128 * (i + 1)] for i in range(4))
    step = softplus(dot3(n2, sp2_p, mmt) + halves(vm["sb2"][...]))
    cum = exact_left(mask_bf(tri_r >= tri_c), -halves(vm["ra2"][...]) * step)
    end = cum[T - 1 : T]
    stepped = inner * step
    write_t2 = split2(write.T)
    state = dot3(write_t2, stepped * jnp.exp(end - cum))
    own_d = jnp.exp(end)
    st, e1s, e1r = sc["st"], sc["e1s"], sc["e1r"]
    st[...] = state
    e1s[0:64] = st[pl.ds(pl.multiple_of(64 * (1 - c), 64), 64), :]
    e1s[64:72] = jnp.broadcast_to(own_d, (8, 128))
    e1 = remote(e1s, e1r, {"seq": seq_of(x, z, 1 - c)})
    e1.start()
    own_half = st[pl.ds(pl.multiple_of(64 * c, 64), 64), :]

    read2 = split2(read)
    pairs = dot3(read2, write_t2)
    cum_t = cum.T
    allowed = tri_r >= tri_c
    local = halves(vm["sk2"][...]) * inner
    first = iota((T, 128), 1) < 64
    for h in range(2):
        diff = cum[:, 64 * h : 64 * h + 1] - cum_t[64 * h : 64 * h + 1, :]
        wts = jnp.where(allowed, jnp.exp(jnp.where(allowed, diff, 0.0)) * pairs, 0.0)
        local = local + dot3(wts, jnp.where(first if h == 0 else ~first, stepped, 0.0))
    gate_s = silu(gate)

    e1.wait_recv()
    got, got_d = e1r[0:64], e1r[64:65]
    s0, s1_ = pick(c, got, own_half), pick(c, own_half, got)
    d0, d1 = pick(c, got_d, own_d), pick(c, own_d, got_d)
    tot, dec = d1 * s0 + s1_, d0 * d1
    pre, pre_d = jnp.zeros((64, 128), F32), jnp.ones((1, 128), F32)
    rounds = []
    for r in range(3):
        bs, br = sc["bs"].at[r], sc["br"].at[r]
        bs[0:64] = tot
        bs[64:72] = jnp.broadcast_to(dec, (8, 128))
        cp = remote(bs, br, {"seq": seq_of(x, xor(z, 1 << r, 3), c)})
        cp.start()
        rounds.append(cp)
        cp.wait_recv()
        got, got_d = br[0:64], br[64:65]
        later = z // (1 << r) % 2
        pre, pre_d = pick(later, pre_d * got + pre, pre), pick(later, got_d * pre_d, pre_d)
        tot = pick(later, dec * got + tot, got_d * tot + got)
        dec = dec * got_d
    xs, xr = sc["xs"], sc["xr"]
    xs[0:64] = tot
    xs[64:72] = jnp.broadcast_to(dec, (8, 128))
    x_copies = [remote(xs, xr.at[x], {"seq": seq_of(xor(x, k, 2), z, c)}) for k in range(1, NX)]
    for cp in x_copies:
        cp.start()
    xr[pl.ds(x, 1)] = xs[...][None]
    for cp in x_copies:
        cp.wait_recv()
    row_in = jnp.zeros((64, 128), F32)
    for i in range(NX - 1):
        row_in = pick(as_int(x > i), xr[i, 64:65] * row_in + xr[i, 0:64], row_in)
    k0 = pre_d * row_in + pre
    k1 = d0 * k0 + s0
    ks, kr = sc["ks"], sc["kr"]
    ks[...] = pick(c, k0, k1)
    k_copy = remote(ks, kr, {"seq": seq_of(x, z, 1 - c)})
    k_copy.start()
    mine = pick(c, k1, k0)
    k_copy.wait_recv()
    got = kr[...]
    carried = jnp.concatenate([pick(c, got, mine), pick(c, mine, got)], axis=0)
    y2 = local + dot3(read2, carried) * jnp.exp(cum)
    w = y2 * gate_s
    gs, gr = sc["gs"], sc["gr"]
    gs[...] = w * head_scale(w) * vm["on2"][...]

    def share_of(ref, p):
        return ref.at[pl.ds(pl.multiple_of(64 * p, 64), 64), :]

    g_copies = [remote(share_of(gs, p), gr.at[y], {"head": p}) for p in y_peers]
    for cp in g_copies:
        cp.start()
    gr[pl.ds(y, 1)] = share_of(gs, y)[...][None]
    for cp in wo2_copies:
        cp.wait_recv()
    out = share_of(mir, y)[...]
    wo2 = [split2(sc["wo2"][i]) for i in range(NY)]
    for cp in g_copies:
        cp.wait_recv()
    for i in range(NY):
        out = out + dot3(gr[i], wo2[i])
    out_ref[...] = out

    for cp in (
        tab_copies + tok_copies + [tokm_copy] + wo1_copies + wo2_copies + z_copies
        + [e1] + rounds + x_copies + [k_copy] + g_copies
    ):
        cp.wait_send()


def per_device(*args):
    a = dict(zip(NAMES, args))
    for n in ("sp1", "sp2"):
        a[n] = a[n].T
    flat = [a[n].reshape(s) for n, s in zip(NAMES, SHAPES)]
    return pl.pallas_call(
        kernel,
        out_shape=jax.ShapeDtypeStruct((64, 256), F32),
        in_specs=[pl.BlockSpec(memory_space=pl.ANY)] * N_IN,
        out_specs=pl.BlockSpec(memory_space=pltpu.VMEM),
        scratch_shapes=[pltpu.VMEM(s, t) for s, t in zip(SHAPES, TYPES)]
        + [pltpu.VMEM(s, t) for _, s, t in SCRATCH]
        + [
            pltpu.SemaphoreType.DMA((N_IN + 1,)),
            pltpu.SemaphoreType.DMA((N_SEND,)),
            pltpu.SemaphoreType.DMA((N_SEND,)),
        ],
        compiler_params=pltpu.CompilerParams(
            collective_id=0, has_side_effects=True, vmem_limit_bytes=48 * 2**20
        ),
    )(*flat)


def solution(mesh):
    tokens = P(("rep", "seq"))
    layer = (P(), P(None, None, "head"), P(), P(None, "head")) + (P("head"),) * 4 + (P("head", None),)
    in_specs = (tokens, P(), P()) + layer + layer
    return jax.shard_map(
        per_device,
        mesh=mesh,
        in_specs=in_specs,
        out_specs=P(("rep", "seq", "head"), None),
        check_vma=False,
    )
```

time: 308 us -> 61.7 us (0.20)
  the two profiles are of different devices: /device:TPU:6 before, /device:TPU:1 now
where the time goes in v1:
time: 61.7 us; the launch traced here: 61.4 us
  Pallas kernels  54.3 us (88%)
  local copies, waits for them, and re-layouts  7.01 us (11%)
    pallas_call x1, Pallas kernels, per_device(): pl.pallas_call(kernel, out_shape=jax.ShapeDtypeStruct((64, 256), F32), in...  54.3 us
    unnamed x43, local copies, waits for them, and re-layouts  7.01 us

profile of v1, /device:TPU:1, one launch (start us, length us, event | category | flops | bytes accessed | tf_op | source)
XLA Modules:
  0.0 61.4 jit_solution(6523528497359460239)
XLA Ops:
  0.0 0.0 copy-start.6
  0.0 0.0 copy-start.19
  0.0 0.0 copy-start.20
  0.0 0.0 copy-start.15
  0.0 0.0 copy-start.16
  0.0 0.0 copy-start.17
  0.0 0.0 copy-start.18
  0.0 0.0 copy-start.12
  0.1 0.0 copy-start.14
  0.1 0.0 copy-start.10
  0.1 0.0 copy-start.11
  0.1 0.0 copy-start.8
  0.1 0.0 copy-start.7
  0.1 0.0 copy-start.9
  0.1 0.0 copy-start.13
  0.1 0.6 copy-done.6
  0.7 0.0 copy-done.19
  0.7 0.0 copy-done.20
  0.7 0.0 copy-done.15
  0.7 0.0 copy-done.16
  0.7 0.0 copy-done.17
  0.7 0.0 copy-done.18
  0.8 0.0 copy-done.12
  0.8 0.0 copy-done.14
  0.8 0.0 copy-done.10
  0.8 0.0 copy-done.11
  0.8 0.0 copy-done.8
  0.9 0.0 copy-done.7
  0.9 0.0 copy-done.9
  0.9 0.0 copy-done.13
  0.9 0.0 copy-start
  0.9 0.9 %copy-done = f32[256,2,128]{2,1,0:T(2,128)S(1)} copy-done((f32[256,2,128]{2,1,0:T(2,128)S(1)}, f32[256,2,128]{2,1,0:T(2,128)}, u32[]{:S(2)}) %copy-start) | copy-done | bytes 262168
  1.8 0.0 copy-start.1
  1.8 0.9 %copy-done.1 = f32[256,2,128]{2,1,0:T(2,128)S(1)} copy-done((f32[256,2,128]{2,1,0:T(2,128)S(1)}, f32[256,2,128]{2,1,0:T(2,128)}, u32[]{:S(2)}) %copy-start.1) | copy-done | bytes 262168
  2.8 0.0 copy-start.2
  2.8 0.9 %copy-done.2 = f32[256,2,128]{2,1,0:T(2,128)S(1)} copy-done((f32[256,2,128]{2,1,0:T(2,128)S(1)}, f32[256,2,128]{2,1,0:T(2,128)}, u32[]{:S(2)}) %copy-start.2) | copy-done | bytes 262168
  3.7 0.0 copy-start.3
  3.7 0.9 %copy-done.3 = f32[256,2,128]{2,1,0:T(2,128)S(1)} copy-done((f32[256,2,128]{2,1,0:T(2,128)S(1)}, f32[256,2,128]{2,1,0:T(2,128)}, u32[]{:S(2)}) %copy-start.3) | copy-done | bytes 262168
  4.7 0.0 copy-start.4
  4.7 0.9 %copy-done.4 = f32[128,256]{1,0:T(8,128)S(1)} copy-done((f32[128,256]{1,0:T(8,128)S(1)}, f32[128,256]{1,0:T(8,128)}, u32[]{:S(2)}) %copy-start.4) | copy-done | bytes 131096
  5.6 0.0 copy-start.5
  5.6 0.9 %copy-done.5 = f32[128,256]{1,0:T(8,128)S(1)} copy-done((f32[128,256]{1,0:T(8,128)S(1)}, f32[128,256]{1,0:T(8,128)}, u32[]{:S(2)}) %copy-start.5) | copy-done | bytes 131096
  6.5 54.3 %shard_map.199 = f32[64,256]{1,0:T(8,128)S(1)} custom-call(s32[1,256]{1,0:T(1,128)S(1)} %bitcast.24, f32[16,256]{1,0:T(8,128)S(1)} %copy-done.6, s32[1,256]{1,0:T(1,128)S(1)} %bitcast.25, f32[1,256]{1,0:T(1,128)S(1)} %bitcast.26, f32[512,128]{1,0:T(8,128)S(1)} %bitcast.18, f32[512,128]{1,0:T(8,128)S(1)} %bitcast.19, f32[2,256]{1,0:T(2,128)S(1)} %bitcast.22, ...), custom_call_target="tpu_custom_call" | custom-call | tf_op jit(solution)/shard_map/pallas_call | solution.py:512
  60.8 0.6 %copy.23 = f32[64,256]{1,0:T(8,128)} copy(f32[64,256]{1,0:T(8,128)S(1)} %shard_map.199) | data formatting | bytes 131072
Async XLA Ops:
  0.0 0.7 %copy-start.6 = (f32[16,256]{1,0:T(8,128)S(1)}, f32[16,256]{1,0:T(8,128)}, u32[]{:S(2)}) copy-start(f32[16,256]{1,0:T(8,128)} %refs_1_.1) | copy-start | bytes 49156
  0.0 0.7 %copy-start.19 = (f32[2]{0:T(128)S(1)}, f32[2]{0:T(128)}, u32[]{:S(2)}) copy-start(f32[2]{0:T(128)} %param.39) | copy-start | bytes 28
  0.0 0.7 %copy-start.20 = (f32[128]{0:T(128)S(1)}, f32[128]{0:T(128)}, u32[]{:S(2)}) copy-start(f32[128]{0:T(128)} %param.40) | copy-start | bytes 1540
  0.0 0.7 %copy-start.15 = (f32[2]{0:T(128)S(1)}, f32[2]{0:T(128)}, u32[]{:S(2)}) copy-start(f32[2]{0:T(128)} %param.30) | copy-start | bytes 28
  0.0 0.7 %copy-start.16 = (f32[128]{0:T(128)S(1)}, f32[128]{0:T(128)}, u32[]{:S(2)}) copy-start(f32[128]{0:T(128)} %param.31) | copy-start | bytes 1540
  0.0 0.7 %copy-start.17 = (f32[2]{0:T(128)S(1)}, f32[2]{0:T(128)}, u32[]{:S(2)}) copy-start(f32[2]{0:T(128)} %param.37) | copy-start | bytes 28
  0.0 0.7 %copy-start.18 = (f32[2]{0:T(128)S(1)}, f32[2]{0:T(128)}, u32[]{:S(2)}) copy-start(f32[2]{0:T(128)} %param.38) | copy-start | bytes 28
  0.0 0.7 %copy-start.12 = (f32[256]{0:T(256)S(1)}, f32[256]{0:T(256)}, u32[]{:S(2)}) copy-start(f32[256]{0:T(256)} %param.33) | copy-start | bytes 3076
  0.1 0.7 %copy-start.14 = (f32[2]{0:T(128)S(1)}, f32[2]{0:T(128)}, u32[]{:S(2)}) copy-start(f32[2]{0:T(128)} %param.29) | copy-start | bytes 28
  0.1 0.8 %copy-start.10 = (s32[256]{0:T(256)S(1)}, s32[256]{0:T(256)}, u32[]{:S(2)}) copy-start(s32[256]{0:T(256)} %param.23) | copy-start | bytes 3076
  0.1 0.8 %copy-start.11 = (f32[256]{0:T(256)S(1)}, f32[256]{0:T(256)}, u32[]{:S(2)}) copy-start(f32[256]{0:T(256)} %param.24) | copy-start | bytes 3076
  0.1 0.8 %copy-start.8 = (f32[256,2]{0,1:T(2,128)S(1)}, f32[256,2]{0,1:T(2,128)}, u32[]{:S(2)}) copy-start(f32[256,2]{0,1:T(2,128)} %param.36) | copy-start | bytes 6148
  0.1 0.8 %copy-start.7 = (f32[256,2]{0,1:T(2,128)S(1)}, f32[256,2]{0,1:T(2,128)}, u32[]{:S(2)}) copy-start(f32[256,2]{0,1:T(2,128)} %param.27) | copy-start | bytes 6148
  0.1 0.8 %copy-start.9 = (s32[256]{0:T(256)S(1)}, s32[256]{0:T(256)}, u32[]{:S(2)}) copy-start(s32[256]{0:T(256)} %param.21) | copy-start | bytes 3076
  0.1 0.8 %copy-start.13 = (f32[2]{0:T(128)S(1)}, f32[2]{0:T(128)}, u32[]{:S(2)}) copy-start(f32[2]{0:T(128)} %param.28) | copy-start | bytes 28
  0.9 1.0 %copy-start = (f32[256,2,128]{2,1,0:T(2,128)S(1)}, f32[256,2,128]{2,1,0:T(2,128)}, u32[]{:S(2)}) copy-start(f32[256,2,128]{2,1,0:T(2,128)} %param.25) | copy-start | bytes 786436
  1.8 0.9 %copy-start.1 = (f32[256,2,128]{2,1,0:T(2,128)S(1)}, f32[256,2,128]{2,1,0:T(2,128)}, u32[]{:S(2)}) copy-start(f32[256,2,128]{2,1,0:T(2,128)} %param.26) | copy-start | bytes 786436
  2.8 0.9 %copy-start.2 = (f32[256,2,128]{2,1,0:T(2,128)S(1)}, f32[256,2,128]{2,1,0:T(2,128)}, u32[]{:S(2)}) copy-start(f32[256,2,128]{2,1,0:T(2,128)} %param.34) | copy-start | bytes 786436
  3.7 0.9 %copy-start.3 = (f32[256,2,128]{2,1,0:T(2,128)S(1)}, f32[256,2,128]{2,1,0:T(2,128)}, u32[]{:S(2)}) copy-start(f32[256,2,128]{2,1,0:T(2,128)} %param.35) | copy-start | bytes 786436
  4.7 0.9 %copy-start.4 = (f32[128,256]{1,0:T(8,128)S(1)}, f32[128,256]{1,0:T(8,128)}, u32[]{:S(2)}) copy-start(f32[128,256]{1,0:T(8,128)} %refs_11_.1) | copy-start | bytes 393220
  5.6 0.9 %copy-start.5 = (f32[128,256]{1,0:T(8,128)S(1)}, f32[128,256]{1,0:T(8,128)}, u32[]{:S(2)}) copy-start(f32[128,256]{1,0:T(8,128)} %refs_20_.1) | copy-start | bytes 393220

commit v2 on v1

--- a/solution.py
+++ b/solution.py
@@ -39,9 +39,15 @@
     return f(ah, bh) + (f(ah, bl) + f(al, bh))
 
 
+def dot3_short(a, b):
+    ah, al = a if isinstance(a, tuple) else split2(a)
+    bh, bl = b if isinstance(b, tuple) else split2(b)
+    return mm(jnp.concatenate([ah, al], axis=1), jnp.concatenate([bh, bh], axis=0)) + mm(ah, bl)
+
+
 def exact_left(a, b):
-    h, m, l = split3(b)
-    return mm(a, h) + (mm(a, m) + mm(a, l))
+    h, l = split2(b)
+    return mm(a, h) + mm(a, l)
 
 
 def exact_right(a, b):
@@ -113,32 +119,41 @@
 )
 TYPES = (jnp.int32, F32, jnp.int32) + (F32,) * 18
 N_IN = len(NAMES)
-TAB = 80
-MSG = 72
+TAB = 72
+HALF = 32
+MSG = HALF + 8
 
 SCRATCH = (
     ("tokbuf", (8, 1, T), jnp.int32),
     ("tokm", (1, T), jnp.int32),
+    ("lsend", (8, 128), F32),
+    ("ltab", (NY, 8, 128), F32),
     ("tsend", (TAB, 128), F32),
     ("ytab", (NY, TAB, 128), F32),
     ("wo1", (NY, 128, 256), F32),
+    ("wo1s", (128, 256), F32),
     ("wo2", (NY, 128, 256), F32),
     ("ztile", (8, 128), F32),
     ("zbuf", (NZ, 8, 128), F32),
     ("mir", (T, 256), F32),
     ("st", (128, 128), F32),
-    ("e1s", (MSG, 128), F32),
-    ("e1r", (MSG, 128), F32),
-    ("bs", (3, MSG, 128), F32),
-    ("br", (3, MSG, 128), F32),
-    ("xs", (MSG, 128), F32),
-    ("xr", (NX, MSG, 128), F32),
-    ("ks", (64, 128), F32),
-    ("kr", (64, 128), F32),
+    ("e1s", (2, MSG, 128), F32),
+    ("e1r", (2, MSG, 128), F32),
+    ("bs", (6, MSG, 128), F32),
+    ("br", (6, MSG, 128), F32),
+    ("xs", (2, MSG, 128), F32),
+    ("xr", (2, NX, MSG, 128), F32),
+    ("ks", (2, HALF, 128), F32),
+    ("kr", (2, HALF, 128), F32),
+    ("rd", (T, 256), BF),
+    ("loc", (T, 128), F32),
+    ("gat", (T, 128), F32),
+    ("cue", (T, 128), F32),
     ("gs", (T, 128), F32),
+    ("gf", (64, 128), F32),
     ("gr", (NY, 64, 128), F32),
 )
-N_SEND = 64
+N_SEND = 72
 
 
 def kernel(*refs):
@@ -156,9 +171,9 @@
     def seq_of(xi, zi, ci):
         return (xi * NZ + zi) * NC + ci
 
-    y_peers = [xor(y, k, 2) for k in range(1, NY)]
-    xc_peers = [xor(xc, k, 3) for k in range(1, 8)]
-    z_peers = [xor(z, k, 3) for k in range(1, NZ)]
+    y_peers = [xor(y, k, 2) for k in (2, 1, 3)]
+    xc_peers = [xor(xc, k, 3) for k in (4, 5, 2, 3, 6, 7, 1)]
+    z_peers = [xor(z, k, 3) for k in range(NZ - 1, 0, -1)]
     mirror = seq_of(xm, zm, 1 - c)
 
     barrier = pltpu.get_barrier_semaphore()
@@ -221,29 +236,28 @@
         dot3(sp_r, jnp.concatenate([normed] * 8, axis=0), mmt)
         + jnp.where(even, sb[:, 0:1], sb[:, 1:2])
     )
-    tsend = sc["tsend"]
+    lsend, tsend = sc["lsend"], sc["tsend"]
+    lsend[...] = log_r
     tsend[0:16] = step_p * inner_t
     tsend[16:32] = halves(sk) * inner_t
     tsend[32:48] = silu(gate_t)
     tsend[48:64] = log_alt
-    tsend[64:72] = log_r
-    tsend[72:80] = jnp.broadcast_to(vm["on1"][...], (8, 128))
+    tsend[64:72] = jnp.broadcast_to(vm["on1"][...], (8, 128))
     g_tab = dot3(read_t, jnp.concatenate([write_t] * 8, axis=0), mmt)
 
     pl.semaphore_wait(barrier, 18)
 
-    ytab, tokbuf = sc["ytab"], sc["tokbuf"]
+    ltab, ytab, tokbuf = sc["ltab"], sc["ytab"], sc["tokbuf"]
+    log_copies = [remote(lsend, ltab.at[y], {"head": p}) for p in y_peers]
+    tok_copies = [
+        remote(vm["tok"], tokbuf.at[xc], {"seq": seq_of(p // NC, z, p % NC)}) for p in xc_peers
+    ]
+    tokm_copy = remote(vm["tok"], sc["tokm"], {"seq": mirror})
     tab_copies = [remote(tsend, ytab.at[y], {"head": p}) for p in y_peers]
-    tok_copies = [
-        remote(hbm["tok"], tokbuf.at[xc], {"seq": seq_of(p // NC, z, p % NC)}) for p in xc_peers
-    ]
-    tokm_copy = remote(hbm["tok"], sc["tokm"], {"seq": mirror})
-    wo1_copies = [remote(vm["op1"], sc["wo1"].at[y], {"head": p}) for p in y_peers]
-    wo2_copies = [remote(vm["op2"], sc["wo2"].at[y], {"head": p}) for p in y_peers]
-    for cp in tab_copies + tok_copies + [tokm_copy] + wo1_copies + wo2_copies:
+    for cp in log_copies + tok_copies + [tokm_copy] + tab_copies:
         cp.start()
+    ltab[pl.ds(y, 1)] = log_r[None]
     ytab[pl.ds(y, 1)] = tsend[...][None]
-    sc["wo1"][pl.ds(y, 1)] = vm["op1"][...][None]
     sc["wo2"][pl.ds(y, 1)] = vm["op2"][...][None]
 
     tri_r, tri_c = iota((256, 256), 0), iota((256, 256), 1)
@@ -253,27 +267,31 @@
         return jnp.where(cond, one, 0.0 * one).astype(BF)
 
     perm = mask_bf(vm["comp"][...] == tri_r)
-    w2 = vm["ip2"]
-    s2 = vm["sm2"]
-    w2_all = split2(
-        jnp.concatenate(
-            [
-                w2[pl.ds(0, 256, stride=2), :],
-                w2[pl.ds(1, 256, stride=2), :],
-                s2[pl.ds(0, 256, stride=2), :],
-                s2[pl.ds(1, 256, stride=2), :],
-            ],
-            axis=1,
-        )
-    )
-    sp2 = vm["sp2"][...]
+    wo1s = sc["wo1s"]
+    wo1s[...] = exact_right(vm["op1"][...], perm)
+    sc["wo1"][pl.ds(y, 1)] = wo1s[...][None]
+    w2, s2 = vm["ip2"], vm["sm2"]
+    gain = jnp.broadcast_to(vm["pn2"][...], (128, 256)).T
+    w2_early = split2(
+        jnp.concatenate([w2[pl.ds(1, 256, stride=2), :] * gain, s2[pl.ds(0, 256, stride=2), :] * gain], axis=1)
+    )
+    w2_late = split2(
+        jnp.concatenate([w2[pl.ds(0, 256, stride=2), :] * gain, s2[pl.ds(1, 256, stride=2), :] * gain], axis=1)
+    )
+    sp2 = vm["sp2"][...] * vm["pn2"][...]
     sp2_p = split2(jnp.where(r128 < 64, sp2[0:1], sp2[1:2]))
     emb_p = mm(jnp.concatenate(split3(emb), axis=0), perm).astype(BF)
 
     for cp in tok_copies:
         cp.wait_recv()
-    for cp in tab_copies:
-        cp.wait_recv()
+    for cp in log_copies:
+        cp.wait_recv()
+    core_rows = pl.ds(pl.multiple_of(64 * c, 64), 64)
+    wo1_copies = [
+        remote(wo1s.at[core_rows], sc["wo1"].at[y, core_rows], {"head": p}) for p in y_peers
+    ]
+    for cp in wo1_copies:
+        cp.start()
     r16 = iota((V, T), 0)
     onehot = jnp.concatenate([as_int(tokbuf[b] == r16) for b in range(8)], axis=0)
     onehot = onehot.astype(F32).astype(BF)
@@ -284,12 +302,14 @@
         ),
     ).astype(BF)
     row8 = iota((8, 128), 0)
-    log_hv = ytab[0, 64:72]
+    log_hv = ltab[0]
     for i in range(1, NY):
-        log_hv = jnp.where(row8 // 2 == i, ytab[i, 64:72], log_hv)
+        log_hv = jnp.where(row8 // 2 == i, ltab[i], log_hv)
     r64, l64 = iota((64, 128), 0), iota((64, 128), 1)
     log_bd = jnp.where(r64 // 8 == l64 // 16, jnp.concatenate([log_hv] * 8, axis=0), 0.0)
-    cums = exact_right(log_bd, counts)
+    cums = mm(
+        jnp.concatenate(split2(log_bd), axis=1), jnp.concatenate([counts, counts], axis=0)
+    )
     weight = jnp.exp(cums[:, :512])
     weight = jnp.concatenate([weight[:, :256], weight[:, 256:]], axis=0)
     wh, wl = split2(weight)
@@ -329,6 +349,8 @@
     def lanes_of(a, b):
         return jnp.concatenate([ytab[i, a:b] for i in range(NY)], axis=1)
 
+    for cp in tab_copies:
+        cp.wait_recv()
     row16 = iota((V, 128), 0)
     l16 = iota((V, 128), 1)
     log_t = ytab[0, 48:64]
@@ -340,7 +362,7 @@
     inner_rep = jnp.concatenate([lanes_of(0, 16)] * 8, axis=0)
     bd = iota((128, 512), 0) // 16 == iota((128, 512), 1) // 64
     x_bd = split2(jnp.where(bd, inner_rep, 0.0))
-    outnorm_all = lanes_of(72, 73)
+    outnorm_all = lanes_of(64, 65)
     tokm_copy.wait_recv()
     hot_m = as_int(sc["tokm"][...] == r16).astype(F32).astype(BF)
     rev = mask_bf(tri_r + tri_c == T - 1)
@@ -351,16 +373,21 @@
     embedded = taken[:, 1408:]
     up_c, up_p = scan_rows(hot, decay, False)
     dn_c, dn_p = scan_rows(hot, decay, True)
-    for cp in wo1_copies:
-        cp.wait_recv()
-    wo1h, wo1l = split2(sc["wo1"][...].reshape(512, 256))
-    wo1_p = (mm(wo1h, perm).astype(BF), mm(wo1l, perm).astype(BF))
+    other_core = {"seq": seq_of(x, z, 1 - c)}
+    wo1_passed = []
+    for cp, p in zip(wo1_copies, y_peers):
+        cp.wait_recv()
+        half = sc["wo1"].at[p, core_rows]
+        wo1_passed.append(remote(half, half, other_core))
+        wo1_passed[-1].start()
 
     for cp in z_copies:
         cp.wait_recv()
     ls, lr = iota((128, 512), 1), iota((128, 512), 0)
     spread = mask_bf((lr // 16 == ls % 128 // 16) & (lr % 16 == ls // 128))
-    ld_all = exact_right(zbuf[:, 5, :], spread)
+    ld_all = mm(
+        jnp.concatenate(split2(zbuf[:, 5, :]), axis=1), jnp.concatenate([spread, spread], axis=0)
+    )
     ld_all = jnp.concatenate([ld_all[:, 128 * i : 128 * i + 128] for i in range(NX)], axis=0)
     qm = xm * NZ + zm
     q, q2 = iota((32, 32), 0), iota((32, 32), 1)
@@ -384,18 +411,21 @@
     carry_b = pick(c, sib_d * carry_b + sib, carry_b)
     coef = jnp.concatenate([up_c + up_p * carry_b, dn_c + dn_p * carry_f], axis=0)
     coef = coef * jnp.concatenate([g_row] * 2, axis=0)
-    ssm = dot3(coef, x_bd)
-
-    same_head = mask_bf(r2 // 64 == l2 // 64)
+    ssm = dot3_short(coef, x_bd)
+
+    same_head = jnp.where(r2 // 64 == l2 // 64, 1.0 / 64, 0.0).astype(BF)
+    same_head = jnp.concatenate([same_head, same_head], axis=0)
 
     def head_scale(w):
         parts = []
         for i in range(w.shape[1] // 128):
-            h, l = split2(w[:, 128 * i : 128 * i + 128] ** 2)
-            parts.append(mm(h, same_head) + mm(l, same_head))
+            parts.append(mm(jnp.concatenate(split2(w[:, 128 * i : 128 * i + 128] ** 2), axis=1), same_head))
         sq = parts[0] if len(parts) == 1 else jnp.concatenate(parts, axis=1)
-        return lax.rsqrt(sq * (1.0 / 64) + EPS)
-
+        return lax.rsqrt(sq + EPS)
+
+    for cp in wo1_passed:
+        cp.wait_recv()
+    wo1_p = split2(sc["wo1"][...].reshape(512, 256))
     w_up = (ssm[:T] + skip_x) * silu_g
     w_dn = (ssm[T:] + skip_x) * silu_g
     mixed = (w_up * head_scale(w_up) + w_dn * head_scale(w_dn)) * outnorm_all
@@ -403,10 +433,11 @@
     mir = sc["mir"]
     mir[...] = mirrored
 
-    n2 = split2(rms(mirrored, vm["pn2"][...]))
-    both = dot3(n2, w2_all)
-    gate, inner, write, read = (both[:, 128 * i : 128 * (i + 1)] for i in range(4))
-    step = softplus(dot3(n2, sp2_p, mmt) + halves(vm["sb2"][...]))
+    n2 = split2(mirrored)
+    rms2 = lax.rsqrt(jnp.mean(mirrored * mirrored, axis=-1, keepdims=True) + EPS)
+    step = softplus(dot3(n2, sp2_p, mmt) * rms2 + halves(vm["sb2"][...]))
+    both = dot3(n2, w2_early) * rms2
+    inner, write = both[:, :128], both[:, 128:]
     cum = exact_left(mask_bf(tri_r >= tri_c), -halves(vm["ra2"][...]) * step)
     end = cum[T - 1 : T]
     stepped = inner * step
@@ -415,91 +446,135 @@
     own_d = jnp.exp(end)
     st, e1s, e1r = sc["st"], sc["e1s"], sc["e1r"]
     st[...] = state
-    e1s[0:64] = st[pl.ds(pl.multiple_of(64 * (1 - c), 64), 64), :]
-    e1s[64:72] = jnp.broadcast_to(own_d, (8, 128))
-    e1 = remote(e1s, e1r, {"seq": seq_of(x, z, 1 - c)})
-    e1.start()
-    own_half = st[pl.ds(pl.multiple_of(64 * c, 64), 64), :]
-
+    chunks = range(2)
+
+    def fill(buf, rows, decay):
+        buf[0:HALF] = rows
+        buf[HALF:MSG] = jnp.broadcast_to(decay, (8, 128))
+
+    def part(core, i):
+        return st[pl.ds(pl.multiple_of(64 * core + HALF * i, HALF), HALF), :]
+
+    e1 = []
+    for i in chunks:
+        fill(e1s.at[i], part(1 - c, i), own_d)
+        e1.append(remote(e1s.at[i], e1r.at[i], other_core))
+        e1[i].start()
+
+    s0, tot, dec, pre, pre_d = [None] * 2, [None] * 2, [None] * 2, [None] * 2, [None] * 2
+    rounds = [[None] * 2 for _ in range(3)]
+
+    def send_round(r, i):
+        bs, br = sc["bs"].at[2 * r + i], sc["br"].at[2 * r + i]
+        fill(bs, tot[i], dec[i])
+        rounds[r][i] = remote(bs, br, {"seq": seq_of(x, xor(z, 1 << r, 3), c)})
+        rounds[r][i].start()
+
+    for i in chunks:
+        own = part(c, i)
+        e1[i].wait_recv()
+        got, got_d = e1r[i, 0:HALF], e1r[i, HALF : HALF + 1]
+        s0[i], s1_ = pick(c, got, own), pick(c, own, got)
+        d0, d1 = pick(c, got_d, own_d), pick(c, own_d, got_d)
+        tot[i], dec[i] = d1 * s0[i] + s1_, d0 * d1
+        pre[i], pre_d[i] = jnp.zeros((HALF, 128), F32), jnp.ones((1, 128), F32)
+        send_round(0, i)
+
+    wo2_copies = [remote(vm["op2"], sc["wo2"].at[y], {"head": p}) for p in y_peers]
+    for cp in wo2_copies:
+        cp.start()
+    both = dot3(n2, w2_late) * rms2
+    gate, read = both[:, :128], both[:, 128:]
     read2 = split2(read)
-    pairs = dot3(read2, write_t2)
+    sc["rd"][...] = jnp.concatenate(read2, axis=1)
+    pairs = dot3_short(read2, write_t2)
     cum_t = cum.T
     allowed = tri_r >= tri_c
     local = halves(vm["sk2"][...]) * inner
     first = iota((T, 128), 1) < 64
-    for h in range(2):
-        diff = cum[:, 64 * h : 64 * h + 1] - cum_t[64 * h : 64 * h + 1, :]
-        wts = jnp.where(allowed, jnp.exp(jnp.where(allowed, diff, 0.0)) * pairs, 0.0)
-        local = local + dot3(wts, jnp.where(first if h == 0 else ~first, stepped, 0.0))
-    gate_s = silu(gate)
-
-    e1.wait_recv()
-    got, got_d = e1r[0:64], e1r[64:65]
-    s0, s1_ = pick(c, got, own_half), pick(c, own_half, got)
-    d0, d1 = pick(c, got_d, own_d), pick(c, own_d, got_d)
-    tot, dec = d1 * s0 + s1_, d0 * d1
-    pre, pre_d = jnp.zeros((64, 128), F32), jnp.ones((1, 128), F32)
-    rounds = []
+    xs, xr = sc["xs"], sc["xr"]
+    x_copies = [[], []]
     for r in range(3):
-        bs, br = sc["bs"].at[r], sc["br"].at[r]
-        bs[0:64] = tot
-        bs[64:72] = jnp.broadcast_to(dec, (8, 128))
-        cp = remote(bs, br, {"seq": seq_of(x, xor(z, 1 << r, 3), c)})
-        cp.start()
-        rounds.append(cp)
-        cp.wait_recv()
-        got, got_d = br[0:64], br[64:65]
         later = z // (1 << r) % 2
-        pre, pre_d = pick(later, pre_d * got + pre, pre), pick(later, got_d * pre_d, pre_d)
-        tot = pick(later, dec * got + tot, got_d * tot + got)
-        dec = dec * got_d
-    xs, xr = sc["xs"], sc["xr"]
-    xs[0:64] = tot
-    xs[64:72] = jnp.broadcast_to(dec, (8, 128))
-    x_copies = [remote(xs, xr.at[x], {"seq": seq_of(xor(x, k, 2), z, c)}) for k in range(1, NX)]
-    for cp in x_copies:
-        cp.start()
-    xr[pl.ds(x, 1)] = xs[...][None]
-    for cp in x_copies:
-        cp.wait_recv()
-    row_in = jnp.zeros((64, 128), F32)
-    for i in range(NX - 1):
-        row_in = pick(as_int(x > i), xr[i, 64:65] * row_in + xr[i, 0:64], row_in)
-    k0 = pre_d * row_in + pre
-    k1 = d0 * k0 + s0
+        for i in chunks:
+            rounds[r][i].wait_recv()
+            got, got_d = sc["br"][2 * r + i, 0:HALF], sc["br"][2 * r + i, HALF : HALF + 1]
+            tot[i] = pick(later, dec[i] * got + tot[i], got_d * tot[i] + got)
+            dec[i] = dec[i] * got_d
+            if r < 2:
+                send_round(r + 1, i)
+            else:
+                fill(xs.at[i], tot[i], dec[i])
+                x_copies[i] = [
+                    remote(xs.at[i], xr.at[i, x], {"seq": seq_of(xor(x, k, 2), z, c)})
+                    for k in (2, 1, 3)
+                ]
+                for cp in x_copies[i]:
+                    cp.start()
+                xr[i, pl.ds(x, 1)] = xs[i][None]
+            pre[i] = pick(later, pre_d[i] * got + pre[i], pre[i])
+            pre_d[i] = pick(later, got_d * pre_d[i], pre_d[i])
+        if r < 2:
+            h = r
+            diff = cum[:, 64 * h : 64 * h + 1] - cum_t[64 * h : 64 * h + 1, :]
+            wts = jnp.where(allowed, jnp.exp(jnp.where(allowed, diff, 0.0)) * pairs, 0.0)
+            local = local + dot3(wts, jnp.where(first if h == 0 else ~first, stepped, 0.0))
+    sc["loc"][...] = local
+    sc["gat"][...] = silu(gate)
+    sc["cue"][...] = jnp.exp(cum)
+    for cp in wo2_copies:
+        cp.wait_recv()
     ks, kr = sc["ks"], sc["kr"]
-    ks[...] = pick(c, k0, k1)
-    k_copy = remote(ks, kr, {"seq": seq_of(x, z, 1 - c)})
-    k_copy.start()
-    mine = pick(c, k1, k0)
-    k_copy.wait_recv()
-    got = kr[...]
+    k_copies, mine = [], []
+    for i in chunks:
+        for cp in x_copies[i]:
+            cp.wait_recv()
+        row_in = jnp.zeros((HALF, 128), F32)
+        for n in range(NX - 1):
+            row_in = pick(as_int(x > n), xr[i, n, HALF : HALF + 1] * row_in + xr[i, n, 0:HALF], row_in)
+        k0 = pre_d[i] * row_in + pre[i]
+        k1 = d0 * k0 + s0[i]
+        ks[i] = pick(c, k0, k1)
+        k_copies.append(remote(ks.at[i], kr.at[i], other_core))
+        k_copies[i].start()
+        mine.append(pick(c, k1, k0))
+    for cp in k_copies:
+        cp.wait_recv()
+    got = jnp.concatenate([kr[0], kr[1]], axis=0)
+    mine = jnp.concatenate(mine, axis=0)
     carried = jnp.concatenate([pick(c, got, mine), pick(c, mine, got)], axis=0)
-    y2 = local + dot3(read2, carried) * jnp.exp(cum)
-    w = y2 * gate_s
+    ch, cl = split2(carried)
+    chh = jnp.concatenate([ch, ch], axis=0)
     gs, gr = sc["gs"], sc["gr"]
-    gs[...] = w * head_scale(w) * vm["on2"][...]
-
-    def share_of(ref, p):
-        return ref.at[pl.ds(pl.multiple_of(64 * p, 64), 64), :]
-
-    g_copies = [remote(share_of(gs, p), gr.at[y], {"head": p}) for p in y_peers]
-    for cp in g_copies:
-        cp.start()
-    gr[pl.ds(y, 1)] = share_of(gs, y)[...][None]
-    for cp in wo2_copies:
-        cp.wait_recv()
-    out = share_of(mir, y)[...]
-    wo2 = [split2(sc["wo2"][i]) for i in range(NY)]
-    for cp in g_copies:
-        cp.wait_recv()
-    for i in range(NY):
-        out = out + dot3(gr[i], wo2[i])
+
+    def finish(rows):
+        rd = sc["rd"][rows, :]
+        y2 = sc["loc"][rows, :] + (mm(rd, chh) + mm(rd[:, :128], cl)) * sc["cue"][rows, :]
+        w = y2 * sc["gat"][rows, :]
+        return w * head_scale(w) * vm["on2"][...]
+
+    def rows_of(p):
+        return pl.ds(pl.multiple_of(64 * p, 64), 64)
+
+    far = y_peers[0]
+    gf = sc["gf"]
+    gf[...] = finish(rows_of(far))
+    g_copies = [remote(gf, gr.at[y], {"head": far})]
+    g_copies[0].start()
+    gs[...] = finish(pl.ds(0, T))
+    for p in y_peers[1:]:
+        g_copies.append(remote(gs.at[rows_of(p)], gr.at[y], {"head": p}))
+        g_copies[-1].start()
+    wo2 = sc["wo2"]
+    out = mir[rows_of(y), :] + dot3_short(gs[rows_of(y), :], wo2[y])
+    for cp, p in zip(g_copies[1:] + g_copies[:1], y_peers[1:] + y_peers[:1]):
+        cp.wait_recv()
+        out = out + dot3_short(gr[p], wo2[p])
     out_ref[...] = out
 
     for cp in (
-        tab_copies + tok_copies + [tokm_copy] + wo1_copies + wo2_copies + z_copies
-        + [e1] + rounds + x_copies + [k_copy] + g_copies
+        log_copies + tab_copies + tok_copies + [tokm_copy] + wo1_copies + wo1_passed + wo2_copies + z_copies
+        + e1 + rounds[0] + rounds[1] + rounds[2] + x_copies[0] + x_copies[1] + k_copies + g_copies
     ):
         cp.wait_send()
 
@@ -512,7 +587,7 @@
     return pl.pallas_call(
         kernel,
         out_shape=jax.ShapeDtypeStruct((64, 256), F32),
-        in_specs=[pl.BlockSpec(memory_space=pl.ANY)] * N_IN,
+        in_specs=[pl.BlockSpec(memory_space=pltpu.HBM)] * N_IN,
         out_specs=pl.BlockSpec(memory_space=pltpu.VMEM),
         scratch_shapes=[pltpu.VMEM(s, t) for s, t in zip(SHAPES, TYPES)]
         + [pltpu.VMEM(s, t) for _, s, t in SCRATCH]
@@ -522,7 +597,7 @@
             pltpu.SemaphoreType.DMA((N_SEND,)),
         ],
         compiler_params=pltpu.CompilerParams(
-            collective_id=0, has_side_effects=True, vmem_limit_bytes=48 * 2**20
+            collective_id=0, has_side_effects=True, vmem_limit_bytes=60 * 2**20
         ),
     )(*flat)
 

time: 61.7 us -> 55.1 us (0.89)
  local copies, waits for them, and re-layouts: 7.01 us -> 1.47 us
  Pallas kernels: 54.3 us -> 53.5 us
    unnamed x43 -> x1, local copies, waits for them, and re-layouts: 7.01 us -> 1.47 us
    pallas_call x1, Pallas kernels: 54.3 us -> 53.5 us  [per_device(): pl.pallas_call(kernel, out_shape=jax.ShapeDtypeStruct((64, 256), F32), in...]
where the time goes in v2:
time: 55.1 us; the launch traced here: 54.9 us
  Pallas kernels  53.5 us (97%)
  local copies, waits for them, and re-layouts  1.47 us (3%)
    pallas_call x1, Pallas kernels, per_device(): pl.pallas_call(kernel, out_shape=jax.ShapeDtypeStruct((64, 256), F32), in...  53.5 us
    unnamed x1, local copies, waits for them, and re-layouts  1.47 us

profile of v2, /device:TPU:1, one launch (start us, length us, event | category | flops | bytes accessed | tf_op | source)
XLA Modules:
  0.0 54.9 jit_solution(13741899819009671995)
XLA Ops:
  0.0 53.5 %shard_map.199 = f32[64,256]{1,0:T(8,128)} custom-call(s32[1,256]{1,0:T(1,128)} %bitcast.24, f32[16,256]{1,0:T(8,128)} %refs_1_.1, s32[1,256]{1,0:T(1,128)} %bitcast.25, f32[1,256]{1,0:T(1,128)} %bitcast.26, f32[512,128]{1,0:T(8,128)} %bitcast.18, f32[512,128]{1,0:T(8,128)} %bitcast.19, f32[2,256]{1,0:T(2,128)} %bitcast.22, f32[1,2]{1,0:T(1,128)} %bitcast.28, ...), custom_call_target="tpu_custom_call" | custom-call | tf_op jit(solution)/shard_map/pallas_call | solution.py:587
  53.5 1.5 %copy.23 = f32[64,256]{1,0:T(8,128)} copy(f32[64,256]{1,0:T(8,128)} %shard_map.199) | data formatting | bytes 131072

commit v3 on v2

--- a/solution.py
+++ b/solution.py
@@ -125,6 +125,7 @@
 
 SCRATCH = (
     ("tokbuf", (8, 1, T), jnp.int32),
+    ("tokr", (1, T), jnp.int32),
     ("tokm", (1, T), jnp.int32),
     ("lsend", (8, 128), F32),
     ("ltab", (NY, 8, 128), F32),
@@ -161,7 +162,7 @@
     out_ref = refs[N_IN]
     vm = dict(zip(NAMES, refs[N_IN + 1 :]))
     sc = {s[0]: r for s, r in zip(SCRATCH, refs[N_IN + 1 + N_IN :])}
-    in_sem, send_sem, recv_sem = refs[-3:]
+    in_sem, send_sem, recv_sem, present = refs[-4:]
 
     seq, y = lax.axis_index("seq"), lax.axis_index("head")
     x, z, c = seq // (NZ * NC), seq // NC % NZ, seq % NC
@@ -173,27 +174,30 @@
 
     y_peers = [xor(y, k, 2) for k in (2, 1, 3)]
     xc_peers = [xor(xc, k, 3) for k in (4, 5, 2, 3, 6, 7, 1)]
-    z_peers = [xor(z, k, 3) for k in range(NZ - 1, 0, -1)]
-    mirror = seq_of(xm, zm, 1 - c)
+    z_near = [xor(z, k, 3) for k in (4, 3, 2, 1)]
+    z_far = [xor(z, k, 3) for k in (7, 6, 5)]
 
     barrier = pltpu.get_barrier_semaphore()
 
     def greet(where):
         pl.semaphore_signal(barrier, inc=1, device_id=where, device_id_type=MESH)
 
-    for p in z_peers:
+    for p in z_near:
         greet({"seq": seq_of(x, p, c)})
-    greet({"seq": mirror})
     for p in xc_peers:
         greet({"seq": seq_of(p // NC, z, p % NC)})
     for p in y_peers:
         greet({"head": p})
 
     loads = {n: pltpu.make_async_copy(hbm[n], vm[n], in_sem.at[i]) for i, n in enumerate(NAMES)}
-    for n in NAMES:
+    first_loads = ("tok", "emb", "pn1", "sp1", "sb1", "ra1")
+    for n in first_loads:
         loads[n].start()
     own_tok = pltpu.make_async_copy(hbm["tok"], sc["tokbuf"].at[xc], in_sem.at[N_IN])
     own_tok.start()
+    other_loads = tuple(n for n in NAMES if n not in first_loads)
+    for n in other_loads:
+        loads[n].start()
 
     used = [0]
 
@@ -205,22 +209,46 @@
             device_id=where, device_id_type=MESH,
         )
 
-    for n in NAMES:
+    for n in first_loads:
         loads[n].wait()
+
+    lane = iota((1, 128), 1)
+    emb = vm["emb"][...]
+    normed = rms(emb, vm["pn1"][...])
+    sp, sb, ra = vm["sp1"][...], vm["sb1"][...], vm["ra1"][...]
+    even = iota((8, 128), 0) % 2 == 0
+    sp_r = jnp.where(iota((8, 256), 0) % 2 == 0, sp[0:1], sp[1:2])
+    log_r = -jnp.where(even, ra[:, 0:1], ra[:, 1:2]) * softplus(
+        dot3(sp_r, jnp.concatenate([normed] * 8, axis=0), mmt)
+        + jnp.where(even, sb[:, 0:1], sb[:, 1:2])
+    )
+    lsend, tsend = sc["lsend"], sc["tsend"]
+    lsend[...] = log_r
+
+    pl.semaphore_wait(barrier, 14)
+    pl.semaphore_signal(
+        present, inc=1, device_id={"seq": seq_of(x, z_near[0], c)}, device_id_type=MESH
+    )
+    ltab, ytab, tokbuf = sc["ltab"], sc["ytab"], sc["tokbuf"]
+    log_copies = [remote(lsend, ltab.at[y], {"head": p}) for p in y_peers]
+    tok_copies = [
+        remote(vm["tok"], tokbuf.at[xc], {"seq": seq_of(p // NC, z, p % NC)}) for p in xc_peers
+    ]
+    for cp in log_copies + tok_copies:
+        cp.start()
+    ltab[pl.ds(y, 1)] = log_r[None]
+
     own_tok.wait()
-
-    lane = iota((1, 128), 1)
+    for n in other_loads:
+        loads[n].wait()
     w1 = vm["ip1"]
     gate_w, inner_w = w1[pl.ds(0, 256, stride=2), :], w1[pl.ds(1, 256, stride=2), :]
     s1 = vm["sm1"]
     write_w, read_w = s1[pl.ds(0, 256, stride=2), :], s1[pl.ds(1, 256, stride=2), :]
-    emb = vm["emb"][...]
-    normed = rms(emb, vm["pn1"][...])
     normed2 = split2(normed)
     table = dot3(normed2, jnp.concatenate([gate_w, inner_w, write_w, read_w], axis=1))
     gate_t, inner_t, write_t, read_t = (table[:, 128 * i : 128 * (i + 1)] for i in range(4))
-    sp = vm["sp1"][...]
-    sb, ra, sk = vm["sb1"][...], vm["ra1"][...], vm["sk1"][...]
+    sk = vm["sk1"][...]
     r128 = iota((128, 256), 0)
     sp_p = jnp.where(r128 < 64, sp[0:1], sp[1:2])
     sp_alt = jnp.where(r128 // 16 % 2 == 0, sp[0:1], sp[1:2])
@@ -230,33 +258,15 @@
     log_alt = -jnp.where(alt, ra[:, 0:1], ra[:, 1:2]) * softplus(
         logits[:, 128:] + jnp.where(alt, sb[:, 0:1], sb[:, 1:2])
     )
-    even = iota((8, 128), 0) % 2 == 0
-    sp_r = jnp.where(iota((8, 256), 0) % 2 == 0, sp[0:1], sp[1:2])
-    log_r = -jnp.where(even, ra[:, 0:1], ra[:, 1:2]) * softplus(
-        dot3(sp_r, jnp.concatenate([normed] * 8, axis=0), mmt)
-        + jnp.where(even, sb[:, 0:1], sb[:, 1:2])
-    )
-    lsend, tsend = sc["lsend"], sc["tsend"]
-    lsend[...] = log_r
     tsend[0:16] = step_p * inner_t
     tsend[16:32] = halves(sk) * inner_t
     tsend[32:48] = silu(gate_t)
     tsend[48:64] = log_alt
     tsend[64:72] = jnp.broadcast_to(vm["on1"][...], (8, 128))
+    tab_copies = [remote(tsend, ytab.at[y], {"head": p}) for p in y_peers]
+    for cp in tab_copies:
+        cp.start()
     g_tab = dot3(read_t, jnp.concatenate([write_t] * 8, axis=0), mmt)
-
-    pl.semaphore_wait(barrier, 18)
-
-    ltab, ytab, tokbuf = sc["ltab"], sc["ytab"], sc["tokbuf"]
-    log_copies = [remote(lsend, ltab.at[y], {"head": p}) for p in y_peers]
-    tok_copies = [
-        remote(vm["tok"], tokbuf.at[xc], {"seq": seq_of(p // NC, z, p % NC)}) for p in xc_peers
-    ]
-    tokm_copy = remote(vm["tok"], sc["tokm"], {"seq": mirror})
-    tab_copies = [remote(tsend, ytab.at[y], {"head": p}) for p in y_peers]
-    for cp in log_copies + tok_copies + [tokm_copy] + tab_copies:
-        cp.start()
-    ltab[pl.ds(y, 1)] = log_r[None]
     ytab[pl.ds(y, 1)] = tsend[...][None]
     sc["wo2"][pl.ds(y, 1)] = vm["op2"][...][None]
 
@@ -284,6 +294,8 @@
 
     for cp in tok_copies:
         cp.wait_recv()
+    mirror_relay = remote(tokbuf.at[xm * NC + 1 - c], sc["tokr"], {"seq": seq_of(x, z_near[0], c)})
+    mirror_relay.start()
     for cp in log_copies:
         cp.wait_recv()
     core_rows = pl.ds(pl.multiple_of(64 * c, 64), 64)
@@ -341,7 +353,7 @@
     tile = jnp.concatenate(rows + [own_b, packed, sib, sib_ld], axis=0)
     ztile, zbuf = sc["ztile"], sc["zbuf"]
     ztile[...] = tile
-    z_copies = [remote(ztile, zbuf.at[z], {"seq": seq_of(x, p, c)}) for p in z_peers]
+    z_copies = [remote(ztile, zbuf.at[z], {"seq": seq_of(x, p, c)}) for p in z_near]
     for cp in z_copies:
         cp.start()
     zbuf[pl.ds(z, 1)] = tile[None]
@@ -363,6 +375,21 @@
     bd = iota((128, 512), 0) // 16 == iota((128, 512), 1) // 64
     x_bd = split2(jnp.where(bd, inner_rep, 0.0))
     outnorm_all = lanes_of(64, 65)
+    pl.semaphore_wait(present, 1)
+    far_copies = [remote(ztile, zbuf.at[z], {"seq": seq_of(x, p, c)}) for p in z_far]
+    for cp in far_copies:
+        cp.start()
+    z_copies += far_copies
+    mirror_relay.wait_recv()
+    tokm_copy = remote(sc["tokr"], sc["tokm"], {"seq": seq_of(x, z_near[1], c)})
+    tokm_copy.start()
+    other_core = {"seq": seq_of(x, z, 1 - c)}
+    wo1_passed = []
+    for cp, p in zip(wo1_copies, y_peers):
+        cp.wait_recv()
+        half = sc["wo1"].at[p, core_rows]
+        wo1_passed.append(remote(half, half, other_core))
+        wo1_passed[-1].start()
     tokm_copy.wait_recv()
     hot_m = as_int(sc["tokm"][...] == r16).astype(F32).astype(BF)
     rev = mask_bf(tri_r + tri_c == T - 1)
@@ -373,13 +400,6 @@
     embedded = taken[:, 1408:]
     up_c, up_p = scan_rows(hot, decay, False)
     dn_c, dn_p = scan_rows(hot, decay, True)
-    other_core = {"seq": seq_of(x, z, 1 - c)}
-    wo1_passed = []
-    for cp, p in zip(wo1_copies, y_peers):
-        cp.wait_recv()
-        half = sc["wo1"].at[p, core_rows]
-        wo1_passed.append(remote(half, half, other_core))
-        wo1_passed[-1].start()
 
     for cp in z_copies:
         cp.wait_recv()
@@ -573,7 +593,7 @@
     out_ref[...] = out
 
     for cp in (
-        log_copies + tab_copies + tok_copies + [tokm_copy] + wo1_copies + wo1_passed + wo2_copies + z_copies
+        log_copies + tab_copies + tok_copies + [mirror_relay, tokm_copy] + wo1_copies + wo1_passed + wo2_copies + z_copies
         + e1 + rounds[0] + rounds[1] + rounds[2] + x_copies[0] + x_copies[1] + k_copies + g_copies
     ):
         cp.wait_send()
@@ -595,6 +615,7 @@
             pltpu.SemaphoreType.DMA((N_IN + 1,)),
             pltpu.SemaphoreType.DMA((N_SEND,)),
             pltpu.SemaphoreType.DMA((N_SEND,)),
+            pltpu.SemaphoreType.REGULAR,
         ],
         compiler_params=pltpu.CompilerParams(
             collective_id=0, has_side_effects=True, vmem_limit_bytes=60 * 2**20

time: 55.1 us -> 51.4 us (0.933)
  Pallas kernels: 53.5 us -> 49.7 us
    pallas_call x1, Pallas kernels: 53.5 us -> 49.7 us  [per_device(): pl.pallas_call(kernel, out_shape=jax.ShapeDtypeStruct((64, 256), F32), in...]
where the time goes in v3:
time: 51.4 us; the launch traced here: 51.2 us
  Pallas kernels  49.7 us (97%)
  local copies, waits for them, and re-layouts  1.47 us (3%)
    pallas_call x1, Pallas kernels, per_device(): pl.pallas_call(kernel, out_shape=jax.ShapeDtypeStruct((64, 256), F32), in...  49.7 us
    unnamed x1, local copies, waits for them, and re-layouts  1.47 us

profile of v3, /device:TPU:1, one launch (start us, length us, event | category | flops | bytes accessed | tf_op | source)
XLA Modules:
  0.0 51.2 jit_solution(11121802965801670093)
XLA Ops:
  0.0 49.7 %shard_map.199 = f32[64,256]{1,0:T(8,128)} custom-call(s32[1,256]{1,0:T(1,128)} %bitcast.24, f32[16,256]{1,0:T(8,128)} %refs_1_.1, s32[1,256]{1,0:T(1,128)} %bitcast.25, f32[1,256]{1,0:T(1,128)} %bitcast.26, f32[512,128]{1,0:T(8,128)} %bitcast.18, f32[512,128]{1,0:T(8,128)} %bitcast.19, f32[2,256]{1,0:T(2,128)} %bitcast.22, f32[1,2]{1,0:T(1,128)} %bitcast.28, ...), custom_call_target="tpu_custom_call" | custom-call | tf_op jit(solution)/shard_map/pallas_call | solution.py:607
  49.7 1.5 %copy.23 = f32[64,256]{1,0:T(8,128)} copy(f32[64,256]{1,0:T(8,128)} %shard_map.199) | data formatting | bytes 131072

commit v4 on v3

--- a/solution.py
+++ b/solution.py
@@ -125,7 +125,6 @@
 
 SCRATCH = (
     ("tokbuf", (8, 1, T), jnp.int32),
-    ("tokr", (1, T), jnp.int32),
     ("tokm", (1, T), jnp.int32),
     ("lsend", (8, 128), F32),
     ("ltab", (NY, 8, 128), F32),
@@ -139,7 +138,9 @@
     ("mir", (T, 256), F32),
     ("st", (128, 128), F32),
     ("e1s", (2, MSG, 128), F32),
+    ("e1o", (2, MSG, 128), F32),
     ("e1r", (2, MSG, 128), F32),
+    ("n1r", (NC, 2, MSG, 128), F32),
     ("bs", (6, MSG, 128), F32),
     ("br", (6, MSG, 128), F32),
     ("xs", (2, MSG, 128), F32),
@@ -292,18 +293,23 @@
     sp2_p = split2(jnp.where(r128 < 64, sp2[0:1], sp2[1:2]))
     emb_p = mm(jnp.concatenate(split3(emb), axis=0), perm).astype(BF)
 
-    for cp in tok_copies:
-        cp.wait_recv()
-    mirror_relay = remote(tokbuf.at[xm * NC + 1 - c], sc["tokr"], {"seq": seq_of(x, z_near[0], c)})
-    mirror_relay.start()
-    for cp in log_copies:
-        cp.wait_recv()
     core_rows = pl.ds(pl.multiple_of(64 * c, 64), 64)
     wo1_copies = [
         remote(wo1s.at[core_rows], sc["wo1"].at[y, core_rows], {"head": p}) for p in y_peers
     ]
     for cp in wo1_copies:
         cp.start()
+    for cp in tok_copies:
+        cp.wait_recv()
+    for cp in log_copies:
+        cp.wait_recv()
+    tokm_copy = remote(tokbuf.at[xm * NC + 1 - c], sc["tokm"], {"seq": seq_of(x, zm, c)})
+
+    def meet_far():
+        pl.semaphore_wait(present, 1)
+        tokm_copy.start()
+
+    pl.when(z >= 4)(meet_far)
     r16 = iota((V, T), 0)
     onehot = jnp.concatenate([as_int(tokbuf[b] == r16) for b in range(8)], axis=0)
     onehot = onehot.astype(F32).astype(BF)
@@ -356,6 +362,11 @@
     z_copies = [remote(ztile, zbuf.at[z], {"seq": seq_of(x, p, c)}) for p in z_near]
     for cp in z_copies:
         cp.start()
+    pl.when(z < 4)(meet_far)
+    far_copies = [remote(ztile, zbuf.at[z], {"seq": seq_of(x, p, c)}) for p in z_far]
+    for cp in far_copies:
+        cp.start()
+    z_copies += far_copies
     zbuf[pl.ds(z, 1)] = tile[None]
 
     def lanes_of(a, b):
@@ -375,14 +386,6 @@
     bd = iota((128, 512), 0) // 16 == iota((128, 512), 1) // 64
     x_bd = split2(jnp.where(bd, inner_rep, 0.0))
     outnorm_all = lanes_of(64, 65)
-    pl.semaphore_wait(present, 1)
-    far_copies = [remote(ztile, zbuf.at[z], {"seq": seq_of(x, p, c)}) for p in z_far]
-    for cp in far_copies:
-        cp.start()
-    z_copies += far_copies
-    mirror_relay.wait_recv()
-    tokm_copy = remote(sc["tokr"], sc["tokm"], {"seq": seq_of(x, z_near[1], c)})
-    tokm_copy.start()
     other_core = {"seq": seq_of(x, z, 1 - c)}
     wo1_passed = []
     for cp, p in zip(wo1_copies, y_peers):
@@ -472,14 +475,26 @@
         buf[0:HALF] = rows
         buf[HALF:MSG] = jnp.broadcast_to(decay, (8, 128))
 
+    def sent(ref, i):
+        return ref.at[pl.ds(0, HALF + 1 if i == 0 else HALF)]
+
     def part(core, i):
         return st[pl.ds(pl.multiple_of(64 * core + HALF * i, HALF), HALF), :]
 
-    e1 = []
+    e1o, n1r = sc["e1o"], sc["n1r"]
+    next_same = {"seq": seq_of(x, xor(z, 1, 3), c)}
+    next_other = {"seq": seq_of(x, xor(z, 1, 3), 1 - c)}
+    e1 = [[], []]
     for i in chunks:
         fill(e1s.at[i], part(1 - c, i), own_d)
-        e1.append(remote(e1s.at[i], e1r.at[i], other_core))
-        e1[i].start()
+        fill(e1o.at[i], part(c, i), own_d)
+        e1[i] = [
+            remote(sent(e1s.at[i], i), sent(n1r.at[c, i], i), next_other),
+            remote(sent(e1o.at[i], i), sent(n1r.at[c, i], i), next_same),
+            remote(sent(e1s.at[i], i), sent(e1r.at[i], i), other_core),
+        ]
+        for cp in e1[i]:
+            cp.start()
 
     s0, tot, dec, pre, pre_d = [None] * 2, [None] * 2, [None] * 2, [None] * 2, [None] * 2
     rounds = [[None] * 2 for _ in range(3)]
@@ -487,18 +502,10 @@
     def send_round(r, i):
         bs, br = sc["bs"].at[2 * r + i], sc["br"].at[2 * r + i]
         fill(bs, tot[i], dec[i])
-        rounds[r][i] = remote(bs, br, {"seq": seq_of(x, xor(z, 1 << r, 3), c)})
+        rounds[r][i] = remote(
+            sent(bs, i), sent(br, i), {"seq": seq_of(x, xor(z, 1 << r, 3), c)}
+        )
         rounds[r][i].start()
-
-    for i in chunks:
-        own = part(c, i)
-        e1[i].wait_recv()
-        got, got_d = e1r[i, 0:HALF], e1r[i, HALF : HALF + 1]
-        s0[i], s1_ = pick(c, got, own), pick(c, own, got)
-        d0, d1 = pick(c, got_d, own_d), pick(c, own_d, got_d)
-        tot[i], dec[i] = d1 * s0[i] + s1_, d0 * d1
-        pre[i], pre_d[i] = jnp.zeros((HALF, 128), F32), jnp.ones((1, 128), F32)
-        send_round(0, i)
 
     wo2_copies = [remote(vm["op2"], sc["wo2"].at[y], {"head": p}) for p in y_peers]
     for cp in wo2_copies:
@@ -513,12 +520,27 @@
     local = halves(vm["sk2"][...]) * inner
     first = iota((T, 128), 1) < 64
     xs, xr = sc["xs"], sc["xr"]
+    x_peers = [xor(x, k, 2) for k in (2, 1, 3)]
     x_copies = [[], []]
     for r in range(3):
         later = z // (1 << r) % 2
         for i in chunks:
-            rounds[r][i].wait_recv()
-            got, got_d = sc["br"][2 * r + i, 0:HALF], sc["br"][2 * r + i, HALF : HALF + 1]
+            if r == 0:
+                for cp in e1[i]:
+                    cp.wait_recv()
+                own, got = part(c, i), e1r[i, 0:HALF]
+                s0[i], s1_ = pick(c, got, own), pick(c, own, got)
+                if i == 0:
+                    got_d = e1r[0, HALF : HALF + 1]
+                    d0, d1 = pick(c, got_d, own_d), pick(c, own_d, got_d)
+                    n0, n1 = n1r[0, 0, HALF : HALF + 1], n1r[1, 0, HALF : HALF + 1]
+                    next_d = n0 * n1
+                tot[i], dec[i] = d1 * s0[i] + s1_, d0 * d1
+                pre[i], pre_d[i] = jnp.zeros((HALF, 128), F32), jnp.ones((1, 128), F32)
+                got, got_d = n1 * n1r[0, i, 0:HALF] + n1r[1, i, 0:HALF], next_d
+            else:
+                rounds[r][i].wait_recv()
+                got, got_d = sc["br"][2 * r + i, 0:HALF], sc["br"][2 * r, HALF : HALF + 1]
             tot[i] = pick(later, dec[i] * got + tot[i], got_d * tot[i] + got)
             dec[i] = dec[i] * got_d
             if r < 2:
@@ -526,12 +548,10 @@
             else:
                 fill(xs.at[i], tot[i], dec[i])
                 x_copies[i] = [
-                    remote(xs.at[i], xr.at[i, x], {"seq": seq_of(xor(x, k, 2), z, c)})
-                    for k in (2, 1, 3)
+                    remote(sent(xs.at[i], i), sent(xr.at[i, x], i), {"seq": seq_of(p, z, c)}) for p in x_peers
                 ]
-                for cp in x_copies[i]:
-                    cp.start()
-                xr[i, pl.ds(x, 1)] = xs[i][None]
+                for cp, p in zip(x_copies[i], x_peers):
+                    pl.when(p > x)(cp.start)
             pre[i] = pick(later, pre_d[i] * got + pre[i], pre[i])
             pre_d[i] = pick(later, got_d * pre_d[i], pre_d[i])
         if r < 2:
@@ -547,11 +567,11 @@
     ks, kr = sc["ks"], sc["kr"]
     k_copies, mine = [], []
     for i in chunks:
-        for cp in x_copies[i]:
-            cp.wait_recv()
+        for cp, p in zip(x_copies[i], x_peers):
+            pl.when(p < x)(cp.wait_recv)
         row_in = jnp.zeros((HALF, 128), F32)
         for n in range(NX - 1):
-            row_in = pick(as_int(x > n), xr[i, n, HALF : HALF + 1] * row_in + xr[i, n, 0:HALF], row_in)
+            row_in = pick(as_int(x > n), xr[0, n, HALF : HALF + 1] * row_in + xr[i, n, 0:HALF], row_in)
         k0 = pre_d[i] * row_in + pre[i]
         k1 = d0 * k0 + s0[i]
         ks[i] = pick(c, k0, k1)
@@ -593,10 +613,13 @@
     out_ref[...] = out
 
     for cp in (
-        log_copies + tab_copies + tok_copies + [mirror_relay, tokm_copy] + wo1_copies + wo1_passed + wo2_copies + z_copies
-        + e1 + rounds[0] + rounds[1] + rounds[2] + x_copies[0] + x_copies[1] + k_copies + g_copies
+        log_copies + tab_copies + tok_copies + [tokm_copy] + wo1_copies + wo1_passed + wo2_copies + z_copies
+        + e1[0] + e1[1] + rounds[1] + rounds[2] + k_copies + g_copies
     ):
         cp.wait_send()
+    for i in chunks:
+        for cp, p in zip(x_copies[i], x_peers):
+            pl.when(p > x)(cp.wait_send)
 
 
 def per_device(*args):

time: 51.4 us -> 48.7 us (0.947)
  the two profiles are of different devices: /device:TPU:1 before, /device:TPU:6 now
where the time goes in v4:
time: 48.7 us; the launch traced here: 48.2 us
  Pallas kernels  46.7 us (96%)
  local copies, waits for them, and re-layouts  1.47 us (3%)
    pallas_call x1, Pallas kernels, per_device(): pl.pallas_call(kernel, out_shape=jax.ShapeDtypeStruct((64, 256), F32), in...  46.7 us
    unnamed x1, local copies, waits for them, and re-layouts  1.47 us

profile of v4, /device:TPU:6, one launch (start us, length us, event | category | flops | bytes accessed | tf_op | source)
XLA Modules:
  0.0 48.2 jit_solution(14669367285010878699)
XLA Ops:
  0.0 46.7 %shard_map.199 = f32[64,256]{1,0:T(8,128)} custom-call(s32[1,256]{1,0:T(1,128)} %bitcast.24, f32[16,256]{1,0:T(8,128)} %refs_1_.1, s32[1,256]{1,0:T(1,128)} %bitcast.25, f32[1,256]{1,0:T(1,128)} %bitcast.26, f32[512,128]{1,0:T(8,128)} %bitcast.18, f32[512,128]{1,0:T(8,128)} %bitcast.19, f32[2,256]{1,0:T(2,128)} %bitcast.22, f32[1,2]{1,0:T(1,128)} %bitcast.28, ...), custom_call_target="tpu_custom_call" | custom-call | tf_op jit(solution)/shard_map/pallas_call | solution.py:630
  46.7 1.5 %copy.23 = f32[64,256]{1,0:T(8,128)} copy(f32[64,256]{1,0:T(8,128)} %shard_map.199) | data formatting | bytes 131072

commit v5 on v4

--- a/solution.py
+++ b/solution.py
@@ -155,7 +155,8 @@
     ("gf", (64, 128), F32),
     ("gr", (NY, 64, 128), F32),
 )
-N_SEND = 72
+N_RECV = 24
+N_MORE = 2
 
 
 def kernel(*refs):
@@ -163,7 +164,7 @@
     out_ref = refs[N_IN]
     vm = dict(zip(NAMES, refs[N_IN + 1 :]))
     sc = {s[0]: r for s, r in zip(SCRATCH, refs[N_IN + 1 + N_IN :])}
-    in_sem, send_sem, recv_sem, present = refs[-4:]
+    in_sem, recv_sem, present = refs[-3:]
 
     seq, y = lax.axis_index("seq"), lax.axis_index("head")
     x, z, c = seq // (NZ * NC), seq // NC % NZ, seq % NC
@@ -200,15 +201,33 @@
     for n in other_loads:
         loads[n].start()
 
-    used = [0]
-
-    def remote(src, dst, where):
-        i = used[0]
+    used = [0, 0]
+
+    def next_sems():
         used[0] += 1
+        used[1] += 1
+        return in_sem.at[used[0] - 1], recv_sem.at[used[1] - 1]
+
+    def remote(src, dst, where, sems=None):
+        send, recv = sems or next_sems()
         return pltpu.make_async_remote_copy(
-            src_ref=src, dst_ref=dst, send_sem=send_sem.at[i], recv_sem=recv_sem.at[i],
+            src_ref=src, dst_ref=dst, send_sem=send, recv_sem=recv,
             device_id=where, device_id_type=MESH,
         )
+
+    class Group:
+        def __init__(self, like):
+            self.send, self.recv = self.sems = next_sems()
+            self.like = like
+
+        def start(self, src, dst, where):
+            remote(src, dst, where, self.sems).start()
+
+        def wait_recv(self):
+            pltpu.make_async_copy(self.like, self.like, self.recv).wait()
+
+        def wait_send(self):
+            pltpu.make_async_copy(self.like, self.like, self.send).wait()
 
     for n in first_loads:
         loads[n].wait()
@@ -231,12 +250,12 @@
         present, inc=1, device_id={"seq": seq_of(x, z_near[0], c)}, device_id_type=MESH
     )
     ltab, ytab, tokbuf = sc["ltab"], sc["ytab"], sc["tokbuf"]
-    log_copies = [remote(lsend, ltab.at[y], {"head": p}) for p in y_peers]
-    tok_copies = [
-        remote(vm["tok"], tokbuf.at[xc], {"seq": seq_of(p // NC, z, p % NC)}) for p in xc_peers
-    ]
-    for cp in log_copies + tok_copies:
-        cp.start()
+    log_copies = Group(ltab.at[pl.ds(0, NY - 1)])
+    tok_copies = Group(tokbuf.at[pl.ds(0, 7)])
+    for p in y_peers:
+        log_copies.start(lsend, ltab.at[y], {"head": p})
+    for p in xc_peers:
+        tok_copies.start(vm["tok"], tokbuf.at[xc], {"seq": seq_of(p // NC, z, p % NC)})
     ltab[pl.ds(y, 1)] = log_r[None]
 
     own_tok.wait()
@@ -264,9 +283,9 @@
     tsend[32:48] = silu(gate_t)
     tsend[48:64] = log_alt
     tsend[64:72] = jnp.broadcast_to(vm["on1"][...], (8, 128))
-    tab_copies = [remote(tsend, ytab.at[y], {"head": p}) for p in y_peers]
-    for cp in tab_copies:
-        cp.start()
+    tab_copies = Group(ytab.at[pl.ds(0, NY - 1)])
+    for p in y_peers:
+        tab_copies.start(tsend, ytab.at[y], {"head": p})
     g_tab = dot3(read_t, jnp.concatenate([write_t] * 8, axis=0), mmt)
     ytab[pl.ds(y, 1)] = tsend[...][None]
     sc["wo2"][pl.ds(y, 1)] = vm["op2"][...][None]
@@ -294,15 +313,11 @@
     emb_p = mm(jnp.concatenate(split3(emb), axis=0), perm).astype(BF)
 
     core_rows = pl.ds(pl.multiple_of(64 * c, 64), 64)
-    wo1_copies = [
-        remote(wo1s.at[core_rows], sc["wo1"].at[y, core_rows], {"head": p}) for p in y_peers
-    ]
-    for cp in wo1_copies:
-        cp.start()
-    for cp in tok_copies:
-        cp.wait_recv()
-    for cp in log_copies:
-        cp.wait_recv()
+    wo1_copies = Group(sc["wo1"].at[pl.ds(0, NY - 1), pl.ds(0, 64)])
+    for p in y_peers:
+        wo1_copies.start(wo1s.at[core_rows], sc["wo1"].at[y, core_rows], {"head": p})
+    tok_copies.wait_recv()
+    log_copies.wait_recv()
     tokm_copy = remote(tokbuf.at[xm * NC + 1 - c], sc["tokm"], {"seq": seq_of(x, zm, c)})
 
     def meet_far():
@@ -359,21 +374,18 @@
     tile = jnp.concatenate(rows + [own_b, packed, sib, sib_ld], axis=0)
     ztile, zbuf = sc["ztile"], sc["zbuf"]
     ztile[...] = tile
-    z_copies = [remote(ztile, zbuf.at[z], {"seq": seq_of(x, p, c)}) for p in z_near]
-    for cp in z_copies:
-        cp.start()
+    z_copies = Group(zbuf.at[pl.ds(0, NZ - 1)])
+    for p in z_near:
+        z_copies.start(ztile, zbuf.at[z], {"seq": seq_of(x, p, c)})
     pl.when(z < 4)(meet_far)
-    far_copies = [remote(ztile, zbuf.at[z], {"seq": seq_of(x, p, c)}) for p in z_far]
-    for cp in far_copies:
-        cp.start()
-    z_copies += far_copies
+    for p in z_far:
+        z_copies.start(ztile, zbuf.at[z], {"seq": seq_of(x, p, c)})
     zbuf[pl.ds(z, 1)] = tile[None]
 
     def lanes_of(a, b):
         return jnp.concatenate([ytab[i, a:b] for i in range(NY)], axis=1)
 
-    for cp in tab_copies:
-        cp.wait_recv()
+    tab_copies.wait_recv()
     row16 = iota((V, 128), 0)
     l16 = iota((V, 128), 1)
     log_t = ytab[0, 48:64]
@@ -387,12 +399,11 @@
     x_bd = split2(jnp.where(bd, inner_rep, 0.0))
     outnorm_all = lanes_of(64, 65)
     other_core = {"seq": seq_of(x, z, 1 - c)}
-    wo1_passed = []
-    for cp, p in zip(wo1_copies, y_peers):
-        cp.wait_recv()
+    wo1_passed = Group(sc["wo1"].at[pl.ds(0, NY - 1), pl.ds(0, 64)])
+    wo1_copies.wait_recv()
+    for p in y_peers:
         half = sc["wo1"].at[p, core_rows]
-        wo1_passed.append(remote(half, half, other_core))
-        wo1_passed[-1].start()
+        wo1_passed.start(half, half, other_core)
     tokm_copy.wait_recv()
     hot_m = as_int(sc["tokm"][...] == r16).astype(F32).astype(BF)
     rev = mask_bf(tri_r + tri_c == T - 1)
@@ -404,8 +415,7 @@
     up_c, up_p = scan_rows(hot, decay, False)
     dn_c, dn_p = scan_rows(hot, decay, True)
 
-    for cp in z_copies:
-        cp.wait_recv()
+    z_copies.wait_recv()
     ls, lr = iota((128, 512), 1), iota((128, 512), 0)
     spread = mask_bf((lr // 16 == ls % 128 // 16) & (lr % 16 == ls // 128))
     ld_all = mm(
@@ -446,8 +456,7 @@
         sq = parts[0] if len(parts) == 1 else jnp.concatenate(parts, axis=1)
         return lax.rsqrt(sq + EPS)
 
-    for cp in wo1_passed:
-        cp.wait_recv()
+    wo1_passed.wait_recv()
     wo1_p = split2(sc["wo1"][...].reshape(512, 256))
     w_up = (ssm[:T] + skip_x) * silu_g
     w_dn = (ssm[T:] + skip_x) * silu_g
@@ -484,17 +493,13 @@
     e1o, n1r = sc["e1o"], sc["n1r"]
     next_same = {"seq": seq_of(x, xor(z, 1, 3), c)}
     next_other = {"seq": seq_of(x, xor(z, 1, 3), 1 - c)}
-    e1 = [[], []]
+    e1 = [Group(sc["bs"].at[pl.ds(0, 3), pl.ds(0, HALF + 1 - i)]) for i in chunks]
     for i in chunks:
         fill(e1s.at[i], part(1 - c, i), own_d)
         fill(e1o.at[i], part(c, i), own_d)
-        e1[i] = [
-            remote(sent(e1s.at[i], i), sent(n1r.at[c, i], i), next_other),
-            remote(sent(e1o.at[i], i), sent(n1r.at[c, i], i), next_same),
-            remote(sent(e1s.at[i], i), sent(e1r.at[i], i), other_core),
-        ]
-        for cp in e1[i]:
-            cp.start()
+        e1[i].start(sent(e1s.at[i], i), sent(n1r.at[c, i], i), next_other)
+        e1[i].start(sent(e1o.at[i], i), sent(n1r.at[c, i], i), next_same)
+        e1[i].start(sent(e1s.at[i], i), sent(e1r.at[i], i), other_core)
 
     s0, tot, dec, pre, pre_d = [None] * 2, [None] * 2, [None] * 2, [None] * 2, [None] * 2
     rounds = [[None] * 2 for _ in range(3)]
@@ -507,9 +512,9 @@
         )
         rounds[r][i].start()
 
-    wo2_copies = [remote(vm["op2"], sc["wo2"].at[y], {"head": p}) for p in y_peers]
-    for cp in wo2_copies:
-        cp.start()
+    wo2_copies = Group(sc["wo2"].at[pl.ds(0, NY - 1)])
+    for p in y_peers:
+        wo2_copies.start(vm["op2"], sc["wo2"].at[y], {"head": p})
     both = dot3(n2, w2_late) * rms2
     gate, read = both[:, :128], both[:, 128:]
     read2 = split2(read)
@@ -526,8 +531,7 @@
         later = z // (1 << r) % 2
         for i in chunks:
             if r == 0:
-                for cp in e1[i]:
-                    cp.wait_recv()
+                e1[i].wait_recv()
                 own, got = part(c, i), e1r[i, 0:HALF]
                 s0[i], s1_ = pick(c, got, own), pick(c, own, got)
                 if i == 0:
@@ -562,10 +566,9 @@
     sc["loc"][...] = local
     sc["gat"][...] = silu(gate)
     sc["cue"][...] = jnp.exp(cum)
-    for cp in wo2_copies:
-        cp.wait_recv()
+    wo2_copies.wait_recv()
     ks, kr = sc["ks"], sc["kr"]
-    k_copies, mine = [], []
+    k_copies, mine = Group(kr), []
     for i in chunks:
         for cp, p in zip(x_copies[i], x_peers):
             pl.when(p < x)(cp.wait_recv)
@@ -575,11 +578,9 @@
         k0 = pre_d[i] * row_in + pre[i]
         k1 = d0 * k0 + s0[i]
         ks[i] = pick(c, k0, k1)
-        k_copies.append(remote(ks.at[i], kr.at[i], other_core))
-        k_copies[i].start()
+        k_copies.start(ks.at[i], kr.at[i], other_core)
         mine.append(pick(c, k1, k0))
-    for cp in k_copies:
-        cp.wait_recv()
+    k_copies.wait_recv()
     got = jnp.concatenate([kr[0], kr[1]], axis=0)
     mine = jnp.concatenate(mine, axis=0)
     carried = jnp.concatenate([pick(c, got, mine), pick(c, mine, got)], axis=0)
@@ -613,8 +614,8 @@
     out_ref[...] = out
 
     for cp in (
-        log_copies + tab_copies + tok_copies + [tokm_copy] + wo1_copies + wo1_passed + wo2_copies + z_copies
-        + e1[0] + e1[1] + rounds[1] + rounds[2] + k_copies + g_copies
+        [log_copies, tab_copies, tok_copies, tokm_copy, wo1_copies, wo1_passed, wo2_copies, z_copies]
+        + e1 + rounds[1] + rounds[2] + [k_copies] + g_copies
     ):
         cp.wait_send()
     for i in chunks:
@@ -629,15 +630,14 @@
     flat = [a[n].reshape(s) for n, s in zip(NAMES, SHAPES)]
     return pl.pallas_call(
         kernel,
-        out_shape=jax.ShapeDtypeStruct((64, 256), F32),
+        out_shape=pltpu.VMEM((64, 256), F32),
         in_specs=[pl.BlockSpec(memory_space=pltpu.HBM)] * N_IN,
         out_specs=pl.BlockSpec(memory_space=pltpu.VMEM),
         scratch_shapes=[pltpu.VMEM(s, t) for s, t in zip(SHAPES, TYPES)]
         + [pltpu.VMEM(s, t) for _, s, t in SCRATCH]
         + [
-            pltpu.SemaphoreType.DMA((N_IN + 1,)),
-            pltpu.SemaphoreType.DMA((N_SEND,)),
-            pltpu.SemaphoreType.DMA((N_SEND,)),
+            pltpu.SemaphoreType.DMA((N_IN + 1 + N_MORE,)),
+            pltpu.SemaphoreType.DMA((N_RECV,)),
             pltpu.SemaphoreType.REGULAR,
         ],
         compiler_params=pltpu.CompilerParams(

time: 48.7 us -> 46.1 us (0.947)
  Pallas kernels: 46.7 us -> 44.9 us
  local copies, waits for them, and re-layouts: 1.47 us -> 0.63 us
    pallas_call x1, Pallas kernels: 46.7 us -> 44.9 us  [per_device(): pl.pallas_call(kernel, out_shape=pltpu.VMEM((64, 256), F32), in_specs=[pl...]
    unnamed x1, local copies, waits for them, and re-layouts: 1.47 us -> 0.63 us
where the time goes in v5:
time: 46.1 us; the launch traced here: 45.6 us
  Pallas kernels  44.9 us (97%)
  local copies, waits for them, and re-layouts  0.63 us (1%)
    pallas_call x1, Pallas kernels, per_device(): pl.pallas_call(kernel, out_shape=pltpu.VMEM((64, 256), F32), in_specs=[pl...  44.9 us

profile of v5, /device:TPU:6, one launch (start us, length us, event | category | flops | bytes accessed | tf_op | source)
XLA Modules:
  0.0 45.6 jit_solution(1363667773766450984)
XLA Ops:
  0.0 44.9 %shard_map.199 = f32[64,256]{1,0:T(8,128)S(1)} custom-call(s32[1,256]{1,0:T(1,128)} %bitcast.24, f32[16,256]{1,0:T(8,128)} %refs_1_.1, s32[1,256]{1,0:T(1,128)} %bitcast.25, f32[1,256]{1,0:T(1,128)} %bitcast.26, f32[512,128]{1,0:T(8,128)} %bitcast.18, f32[512,128]{1,0:T(8,128)} %bitcast.19, f32[2,256]{1,0:T(2,128)} %bitcast.22, f32[1,2]{1,0:T(1,128)} %bitcast.28, ...), custom_call_target="tpu_custom_call" | custom-call | tf_op jit(solution)/shard_map/pallas_call | solution.py:631
  44.9 0.6 %copy.23 = f32[64,256]{1,0:T(8,128)} copy(f32[64,256]{1,0:T(8,128)S(1)} %shard_map.199) | data formatting | bytes 131072

commit v6 on v5

--- a/solution.py
+++ b/solution.py
@@ -125,6 +125,7 @@
 
 SCRATCH = (
     ("tokbuf", (8, 1, T), jnp.int32),
+    ("tokr", (4, 1, T), jnp.int32),
     ("tokm", (1, T), jnp.int32),
     ("lsend", (8, 128), F32),
     ("ltab", (NY, 8, 128), F32),
@@ -155,8 +156,8 @@
     ("gf", (64, 128), F32),
     ("gr", (NY, 64, 128), F32),
 )
-N_RECV = 24
-N_MORE = 2
+N_RECV = 29
+N_MORE = 7
 
 
 def kernel(*refs):
@@ -176,16 +177,18 @@
 
     y_peers = [xor(y, k, 2) for k in (2, 1, 3)]
     xc_peers = [xor(xc, k, 3) for k in (4, 5, 2, 3, 6, 7, 1)]
-    z_near = [xor(z, k, 3) for k in (4, 3, 2, 1)]
-    z_far = [xor(z, k, 3) for k in (7, 6, 5)]
+    z_group = [xor(z, k, 3) for k in (3, 2, 1)]
+    low, high, relay, above = z < 4, z >= 4, z == 4, z > 4
 
     barrier = pltpu.get_barrier_semaphore()
 
     def greet(where):
         pl.semaphore_signal(barrier, inc=1, device_id=where, device_id_type=MESH)
 
-    for p in z_near:
+    for p in z_group:
         greet({"seq": seq_of(x, p, c)})
+    pl.when(z == 3)(lambda: greet({"seq": seq_of(x, 4, c)}))
+    pl.when(relay)(lambda: greet({"seq": seq_of(x, 3, c)}))
     for p in xc_peers:
         greet({"seq": seq_of(p // NC, z, p % NC)})
     for p in y_peers:
@@ -206,6 +209,8 @@
     def next_sems():
         used[0] += 1
         used[1] += 1
+        assert used[1] <= N_RECV
+        assert used[0] <= N_IN + 1 + N_MORE
         return in_sem.at[used[0] - 1], recv_sem.at[used[1] - 1]
 
     def remote(src, dst, where, sems=None):
@@ -216,9 +221,10 @@
         )
 
     class Group:
-        def __init__(self, like):
+        def __init__(self, like, sent_like=None):
             self.send, self.recv = self.sems = next_sems()
             self.like = like
+            self.sent_like = like if sent_like is None else sent_like
 
         def start(self, src, dst, where):
             remote(src, dst, where, self.sems).start()
@@ -227,7 +233,7 @@
             pltpu.make_async_copy(self.like, self.like, self.recv).wait()
 
         def wait_send(self):
-            pltpu.make_async_copy(self.like, self.like, self.send).wait()
+            pltpu.make_async_copy(self.sent_like, self.sent_like, self.send).wait()
 
     for n in first_loads:
         loads[n].wait()
@@ -245,10 +251,26 @@
     lsend, tsend = sc["lsend"], sc["tsend"]
     lsend[...] = log_r
 
-    pl.semaphore_wait(barrier, 14)
-    pl.semaphore_signal(
-        present, inc=1, device_id={"seq": seq_of(x, z_near[0], c)}, device_id_type=MESH
-    )
+    def tell(p):
+        pl.semaphore_signal(
+            present, inc=1, device_id={"seq": seq_of(x, p, c)}, device_id_type=MESH
+        )
+
+    across = (z == 3) | relay
+    pl.when(across)(lambda: pl.semaphore_wait(barrier, 14))
+    pl.when(jnp.logical_not(across))(lambda: pl.semaphore_wait(barrier, 13))
+
+    @pl.when(z == 3)
+    def _():
+        for p in (4, 0, 1, 2):
+            tell(p)
+
+    @pl.when(relay)
+    def _():
+        pl.semaphore_wait(present, 1)
+        for p in (7, 6, 5):
+            tell(p)
+
     ltab, ytab, tokbuf = sc["ltab"], sc["ytab"], sc["tokbuf"]
     log_copies = Group(ltab.at[pl.ds(0, NY - 1)])
     tok_copies = Group(tokbuf.at[pl.ds(0, 7)])
@@ -318,13 +340,14 @@
         wo1_copies.start(wo1s.at[core_rows], sc["wo1"].at[y, core_rows], {"head": p})
     tok_copies.wait_recv()
     log_copies.wait_recv()
-    tokm_copy = remote(tokbuf.at[xm * NC + 1 - c], sc["tokm"], {"seq": seq_of(x, zm, c)})
-
-    def meet_far():
-        pl.semaphore_wait(present, 1)
-        tokm_copy.start()
-
-    pl.when(z >= 4)(meet_far)
+    pl.when(jnp.logical_not(across))(lambda: pl.semaphore_wait(present, 1))
+    tokr, tokm = sc["tokr"], sc["tokm"]
+    to_gate = {"seq": seq_of(x, 4, c)}
+    mirror_tok = tokbuf.at[xm * NC + 1 - c]
+    tokm_copy = remote(mirror_tok, tokm, {"seq": seq_of(x, zm, c)})
+    tok_low = Group(tokr, tokr.at[pl.ds(0, 1)])
+    pl.when(high)(tokm_copy.start)
+    pl.when(low)(lambda: tok_low.start(mirror_tok, tokr.at[z], to_gate))
     r16 = iota((V, T), 0)
     onehot = jnp.concatenate([as_int(tokbuf[b] == r16) for b in range(8)], axis=0)
     onehot = onehot.astype(F32).astype(BF)
@@ -374,12 +397,33 @@
     tile = jnp.concatenate(rows + [own_b, packed, sib, sib_ld], axis=0)
     ztile, zbuf = sc["ztile"], sc["zbuf"]
     ztile[...] = tile
-    z_copies = Group(zbuf.at[pl.ds(0, NZ - 1)])
-    for p in z_near:
-        z_copies.start(ztile, zbuf.at[z], {"seq": seq_of(x, p, c)})
-    pl.when(z < 4)(meet_far)
-    for p in z_far:
-        z_copies.start(ztile, zbuf.at[z], {"seq": seq_of(x, p, c)})
+    tiles = zbuf.at[pl.ds(0, 4)]
+    z_own = Group(zbuf.at[pl.ds(0, 3)])
+    z_down = Group(tiles)
+    z_low = Group(tiles, zbuf.at[pl.ds(0, 1)])
+    z_up = Group(tiles, sc["loc"].at[pl.ds(0, 96)])
+    tok_up = Group(tokm, tokr.at[pl.ds(0, 3)])
+    pl.when(low)(lambda: z_low.start(ztile, zbuf.at[z], to_gate))
+
+    @pl.when(high)
+    def _():
+        for p in range(4):
+            z_down.start(ztile, zbuf.at[z], {"seq": seq_of(x, p, c)})
+
+    for p in z_group:
+        z_own.start(ztile, zbuf.at[z], {"seq": seq_of(x, p, c)})
+
+    @pl.when(relay)
+    def _():
+        tok_low.wait_recv()
+        for p in range(3):
+            tok_up.start(tokr.at[p], tokm, {"seq": seq_of(x, NZ - 1 - p, c)})
+        z_low.wait_recv()
+        for p in (7, 6, 5):
+            for n in range(4):
+                z_up.start(zbuf.at[n], zbuf.at[n], {"seq": seq_of(x, p, c)})
+        tokm[...] = tokr[3]
+
     zbuf[pl.ds(z, 1)] = tile[None]
 
     def lanes_of(a, b):
@@ -404,7 +448,8 @@
     for p in y_peers:
         half = sc["wo1"].at[p, core_rows]
         wo1_passed.start(half, half, other_core)
-    tokm_copy.wait_recv()
+    pl.when(low)(tokm_copy.wait_recv)
+    pl.when(above)(tok_up.wait_recv)
     hot_m = as_int(sc["tokm"][...] == r16).astype(F32).astype(BF)
     rev = mask_bf(tri_r + tri_c == T - 1)
     hot_rev = mmt(rev, jnp.concatenate([hot_m] * 3, axis=0)).astype(BF)
@@ -415,7 +460,9 @@
     up_c, up_p = scan_rows(hot, decay, False)
     dn_c, dn_p = scan_rows(hot, decay, True)
 
-    z_copies.wait_recv()
+    z_own.wait_recv()
+    pl.when(low)(z_down.wait_recv)
+    pl.when(above)(z_up.wait_recv)
     ls, lr = iota((128, 512), 1), iota((128, 512), 0)
     spread = mask_bf((lr // 16 == ls % 128 // 16) & (lr % 16 == ls // 128))
     ld_all = mm(
@@ -614,10 +661,14 @@
     out_ref[...] = out
 
     for cp in (
-        [log_copies, tab_copies, tok_copies, tokm_copy, wo1_copies, wo1_passed, wo2_copies, z_copies]
+        [log_copies, tab_copies, tok_copies, wo1_copies, wo1_passed, wo2_copies, z_own]
         + e1 + rounds[1] + rounds[2] + [k_copies] + g_copies
     ):
         cp.wait_send()
+    for cond, cp in (
+        (low, tok_low), (low, z_low), (high, tokm_copy), (high, z_down), (relay, tok_up), (relay, z_up)
+    ):
+        pl.when(cond)(cp.wait_send)
     for i in chunks:
         for cp, p in zip(x_copies[i], x_peers):
             pl.when(p > x)(cp.wait_send)

time: 46.1 us -> 44.8 us (0.972)
  Pallas kernels: 44.9 us -> 43.7 us
    pallas_call x1, Pallas kernels: 44.9 us -> 43.7 us  [per_device(): pl.pallas_call(kernel, out_shape=pltpu.VMEM((64, 256), F32), in_specs=[pl...]
where the time goes in v6:
time: 44.8 us; the launch traced here: 44.4 us
  Pallas kernels  43.7 us (98%)
  local copies, waits for them, and re-layouts  0.63 us (1%)
    pallas_call x1, Pallas kernels, per_device(): pl.pallas_call(kernel, out_shape=pltpu.VMEM((64, 256), F32), in_specs=[pl...  43.7 us

profile of v6, /device:TPU:6, one launch (start us, length us, event | category | flops | bytes accessed | tf_op | source)
XLA Modules:
  0.0 44.4 jit_solution(2675128782615936318)
XLA Ops:
  0.0 43.7 %shard_map.199 = f32[64,256]{1,0:T(8,128)S(1)} custom-call(s32[1,256]{1,0:T(1,128)} %bitcast.24, f32[16,256]{1,0:T(8,128)} %refs_1_.1, s32[1,256]{1,0:T(1,128)} %bitcast.25, f32[1,256]{1,0:T(1,128)} %bitcast.26, f32[512,128]{1,0:T(8,128)} %bitcast.18, f32[512,128]{1,0:T(8,128)} %bitcast.19, f32[2,256]{1,0:T(2,128)} %bitcast.22, f32[1,2]{1,0:T(1,128)} %bitcast.28, ...), custom_call_target="tpu_custom_call" | custom-call | tf_op jit(solution)/shard_map/pallas_call | solution.py:682
  43.7 0.6 %copy.23 = f32[64,256]{1,0:T(8,128)} copy(f32[64,256]{1,0:T(8,128)S(1)} %shard_map.199) | data formatting | bytes 131072

commit v7 on v6

--- a/solution.py
+++ b/solution.py
@@ -156,8 +156,8 @@
     ("gf", (64, 128), F32),
     ("gr", (NY, 64, 128), F32),
 )
-N_RECV = 29
-N_MORE = 7
+N_RECV = 30
+N_MORE = 8
 
 
 def kernel(*refs):
@@ -176,7 +176,7 @@
         return (xi * NZ + zi) * NC + ci
 
     y_peers = [xor(y, k, 2) for k in (2, 1, 3)]
-    xc_peers = [xor(xc, k, 3) for k in (4, 5, 2, 3, 6, 7, 1)]
+    xc_peers = [xor(xc, k, 3) for k in (7, 4, 5, 2, 3, 6, 1)]
     z_group = [xor(z, k, 3) for k in (3, 2, 1)]
     low, high, relay, above = z < 4, z >= 4, z == 4, z > 4
 
@@ -194,13 +194,16 @@
     for p in y_peers:
         greet({"head": p})
 
-    loads = {n: pltpu.make_async_copy(hbm[n], vm[n], in_sem.at[i]) for i, n in enumerate(NAMES)}
     first_loads = ("tok", "emb", "pn1", "sp1", "sb1", "ra1")
+    other_loads = tuple(n for n in NAMES if n not in first_loads)
+    loads = {
+        n: pltpu.make_async_copy(hbm[n], vm[n], in_sem.at[i])
+        for i, n in enumerate(first_loads + other_loads)
+    }
     for n in first_loads:
         loads[n].start()
     own_tok = pltpu.make_async_copy(hbm["tok"], sc["tokbuf"].at[xc], in_sem.at[N_IN])
     own_tok.start()
-    other_loads = tuple(n for n in NAMES if n not in first_loads)
     for n in other_loads:
         loads[n].start()
 
@@ -273,10 +276,12 @@
 
     ltab, ytab, tokbuf = sc["ltab"], sc["ytab"], sc["tokbuf"]
     log_copies = Group(ltab.at[pl.ds(0, NY - 1)])
-    tok_copies = Group(tokbuf.at[pl.ds(0, 7)])
+    tok_first = Group(tokbuf.at[pl.ds(0, 1)])
+    tok_copies = Group(tokbuf.at[pl.ds(0, 6)])
+    tok_first.start(vm["tok"], tokbuf.at[xc], {"seq": seq_of(xc_peers[0] // NC, z, xc_peers[0] % NC)})
     for p in y_peers:
         log_copies.start(lsend, ltab.at[y], {"head": p})
-    for p in xc_peers:
+    for p in xc_peers[1:]:
         tok_copies.start(vm["tok"], tokbuf.at[xc], {"seq": seq_of(p // NC, z, p % NC)})
     ltab[pl.ds(y, 1)] = log_r[None]
 
@@ -319,6 +324,20 @@
         return jnp.where(cond, one, 0.0 * one).astype(BF)
 
     perm = mask_bf(vm["comp"][...] == tri_r)
+    lower_tri = mask_bf(tri_r >= tri_c)
+    count_mat = jnp.concatenate(
+        [mask_bf(tri_r > tri_c), mask_bf(tri_r < tri_c), jnp.ones((256, 128), BF)], axis=1
+    )
+    ls, lr = iota((128, 512), 1), iota((128, 512), 0)
+    spread = mask_bf((lr // 16 == ls % 128 // 16) & (lr % 16 == ls // 128))
+    spread = jnp.concatenate([spread, spread], axis=0)
+    qm = xm * NZ + zm
+    q, q2 = iota((32, 32), 0), iota((32, 32), 1)
+    between = mask_bf(((q2 > q) & (q2 < qm)) | ((q2 < q) & (q2 > qm)))
+    r2, l2 = iota((128, 128), 0), iota((128, 128), 1)
+    same_head = jnp.where(r2 // 64 == l2 // 64, 1.0 / 64, 0.0).astype(BF)
+    same_head = jnp.concatenate([same_head, same_head], axis=0)
+    rev = mask_bf(tri_r + tri_c == T - 1)
     wo1s = sc["wo1s"]
     wo1s[...] = exact_right(vm["op1"][...], perm)
     sc["wo1"][pl.ds(y, 1)] = wo1s[...][None]
@@ -338,8 +357,7 @@
     wo1_copies = Group(sc["wo1"].at[pl.ds(0, NY - 1), pl.ds(0, 64)])
     for p in y_peers:
         wo1_copies.start(wo1s.at[core_rows], sc["wo1"].at[y, core_rows], {"head": p})
-    tok_copies.wait_recv()
-    log_copies.wait_recv()
+    tok_first.wait_recv()
     pl.when(jnp.logical_not(across))(lambda: pl.semaphore_wait(present, 1))
     tokr, tokm = sc["tokr"], sc["tokm"]
     to_gate = {"seq": seq_of(x, 4, c)}
@@ -348,15 +366,12 @@
     tok_low = Group(tokr, tokr.at[pl.ds(0, 1)])
     pl.when(high)(tokm_copy.start)
     pl.when(low)(lambda: tok_low.start(mirror_tok, tokr.at[z], to_gate))
+    tok_copies.wait_recv()
+    log_copies.wait_recv()
     r16 = iota((V, T), 0)
     onehot = jnp.concatenate([as_int(tokbuf[b] == r16) for b in range(8)], axis=0)
     onehot = onehot.astype(F32).astype(BF)
-    counts = mm(
-        onehot,
-        jnp.concatenate(
-            [mask_bf(tri_r > tri_c), mask_bf(tri_r < tri_c), jnp.ones((256, 128), BF)], axis=1
-        ),
-    ).astype(BF)
+    counts = mm(onehot, count_mat).astype(BF)
     row8 = iota((8, 128), 0)
     log_hv = ltab[0]
     for i in range(1, NY):
@@ -370,7 +385,6 @@
     weight = jnp.concatenate([weight[:, :256], weight[:, 256:]], axis=0)
     wh, wl = split2(weight)
     sums = mmt(wh, onehot) + mmt(wl, onehot)
-    r2, l2 = iota((128, 128), 0), iota((128, 128), 1)
     sums = jnp.where(r2 // 8 % 8 == l2 // 16, sums, 0.0)
     for shift in (64, 32, 16):
         sums = sums + pltpu.roll(sums, shift, 1)
@@ -448,10 +462,12 @@
     for p in y_peers:
         half = sc["wo1"].at[p, core_rows]
         wo1_passed.start(half, half, other_core)
+    wo2_copies = Group(sc["wo2"].at[pl.ds(0, NY - 1)])
+    for p in y_peers:
+        wo2_copies.start(vm["op2"], sc["wo2"].at[y], {"head": p})
     pl.when(low)(tokm_copy.wait_recv)
     pl.when(above)(tok_up.wait_recv)
     hot_m = as_int(sc["tokm"][...] == r16).astype(F32).astype(BF)
-    rev = mask_bf(tri_r + tri_c == T - 1)
     hot_rev = mmt(rev, jnp.concatenate([hot_m] * 3, axis=0)).astype(BF)
     taken = mm(hot_rev, tables)
     silu_g, skip_x = taken[:, :512], taken[:, 512:1024]
@@ -463,16 +479,11 @@
     z_own.wait_recv()
     pl.when(low)(z_down.wait_recv)
     pl.when(above)(z_up.wait_recv)
-    ls, lr = iota((128, 512), 1), iota((128, 512), 0)
-    spread = mask_bf((lr // 16 == ls % 128 // 16) & (lr % 16 == ls // 128))
     ld_all = mm(
-        jnp.concatenate(split2(zbuf[:, 5, :]), axis=1), jnp.concatenate([spread, spread], axis=0)
+        jnp.concatenate(split2(zbuf[:, 5, :]), axis=1), spread
     )
     ld_all = jnp.concatenate([ld_all[:, 128 * i : 128 * i + 128] for i in range(NX)], axis=0)
-    qm = xm * NZ + zm
-    q, q2 = iota((32, 32), 0), iota((32, 32), 1)
-    between = ((q2 > q) & (q2 < qm)) | ((q2 < q) & (q2 > qm))
-    share = jnp.exp(exact_left(mask_bf(between), ld_all))
+    share = jnp.exp(exact_left(between, ld_all))
     zrow = iota((8, 128), 0)
     coefs = jnp.concatenate(
         [
@@ -493,9 +504,6 @@
     coef = coef * jnp.concatenate([g_row] * 2, axis=0)
     ssm = dot3_short(coef, x_bd)
 
-    same_head = jnp.where(r2 // 64 == l2 // 64, 1.0 / 64, 0.0).astype(BF)
-    same_head = jnp.concatenate([same_head, same_head], axis=0)
-
     def head_scale(w):
         parts = []
         for i in range(w.shape[1] // 128):
@@ -517,7 +525,7 @@
     step = softplus(dot3(n2, sp2_p, mmt) * rms2 + halves(vm["sb2"][...]))
     both = dot3(n2, w2_early) * rms2
     inner, write = both[:, :128], both[:, 128:]
-    cum = exact_left(mask_bf(tri_r >= tri_c), -halves(vm["ra2"][...]) * step)
+    cum = exact_left(lower_tri, -halves(vm["ra2"][...]) * step)
     end = cum[T - 1 : T]
     stepped = inner * step
     write_t2 = split2(write.T)
@@ -559,9 +567,6 @@
         )
         rounds[r][i].start()
 
-    wo2_copies = Group(sc["wo2"].at[pl.ds(0, NY - 1)])
-    for p in y_peers:
-        wo2_copies.start(vm["op2"], sc["wo2"].at[y], {"head": p})
     both = dot3(n2, w2_late) * rms2
     gate, read = both[:, :128], both[:, 128:]
     read2 = split2(read)
@@ -661,7 +666,7 @@
     out_ref[...] = out
 
     for cp in (
-        [log_copies, tab_copies, tok_copies, wo1_copies, wo1_passed, wo2_copies, z_own]
+        [log_copies, tab_copies, tok_first, tok_copies, wo1_copies, wo1_passed, wo2_copies, z_own]
         + e1 + rounds[1] + rounds[2] + [k_copies] + g_copies
     ):
         cp.wait_send()

time: 44.8 us -> 44.7 us (level)
  no operation moved by 1% of the time
where the time goes in v7:
time: 44.7 us; the launch traced here: 44.3 us
  Pallas kernels  43.6 us (98%)
  local copies, waits for them, and re-layouts  0.63 us (1%)
    pallas_call x1, Pallas kernels, per_device(): pl.pallas_call(kernel, out_shape=pltpu.VMEM((64, 256), F32), in_specs=[pl...  43.6 us

profile of v7, /device:TPU:6, one launch (start us, length us, event | category | flops | bytes accessed | tf_op | source)
XLA Modules:
  0.0 44.3 jit_solution(17374899303833374159)
XLA Ops:
  0.0 43.6 %shard_map.199 = f32[64,256]{1,0:T(8,128)S(1)} custom-call(s32[1,256]{1,0:T(1,128)} %bitcast.24, f32[16,256]{1,0:T(8,128)} %refs_1_.1, s32[1,256]{1,0:T(1,128)} %bitcast.25, f32[1,256]{1,0:T(1,128)} %bitcast.26, f32[512,128]{1,0:T(8,128)} %bitcast.18, f32[512,128]{1,0:T(8,128)} %bitcast.19, f32[2,256]{1,0:T(2,128)} %bitcast.22, f32[1,2]{1,0:T(1,128)} %bitcast.28, ...), custom_call_target="tpu_custom_call" | custom-call | tf_op jit(solution)/shard_map/pallas_call | solution.py:687
  43.6 0.6 %copy.23 = f32[64,256]{1,0:T(8,128)} copy(f32[64,256]{1,0:T(8,128)S(1)} %shard_map.199) | data formatting | bytes 131072
